TPU v7x, 256 devices: a whole 4x4x8 slice. The times are simulated.
256 devices in a mesh: row: 32 (over z, x_hi, core), col: 8 (over y, x_lo).
Axes of the slice: x: 4 (x_hi: 2, x_lo: 2; x = x_hi * 2 + x_lo), y: 4, z: 8, core: 2. Of those that a mesh axis runs over, the one named last changes fastest.
Arguments:
- query_slab: float32 [25600, 64], P(('row', 'col')), may hold values from -6 to 6
- eigenbasis: float32 [25600, 25600], P('row', 'col'), may hold values from -0.0390625 to 0.0390625
- eigenvalues: float32 [25600, 64], P(('col', 'row')), may hold values from 0.02 to 4
- activations: float32 [2048, 25600], P(None, ('row', 'col')), may hold values from -0.15625 to 0.15625
- out_grads: float32 [2048, 64], P(('row', 'col')), may hold values from -0.75 to 0.75
Outputs:
- preconditioned: float32 [25600, 64], P(('row', 'col'))
- scores: float32 [2048], P(('row', 'col'))
All inputs are finite; a program needn't handle non-finite values.
Results may differ from a plain program's by a relative error of at most 0.0003.
Values sent between devices are 32-bit elements; how exact they have to be, the bound alone decides.
A program may use at most 64 MiB of HBM per device.

v0:
```python
import jax
import jax.numpy as jnp
from jax import lax
from jax.sharding import PartitionSpec as P

damping = 0.1


def in_blocks(shard, dim, size):
    dims = shard.shape
    blocks = shard.reshape(*dims[:dim], size, dims[dim] // size, *dims[dim + 1 :])
    return jnp.moveaxis(blocks, dim, 0)


def sent_and_summed(shard, axis, dim):
    size = lax.axis_size(axis)
    blocks = lax.all_to_all(in_blocks(shard, dim, size), axis, 0, 0, tiled=True)
    return jnp.sum(blocks, axis=0)


def from_everyone(shard, axis):
    size = lax.axis_size(axis)
    return lax.all_to_all(
        jnp.broadcast_to(shard[None], (size, *shard.shape)), axis, 0, 0, tiled=True
    )


def laid_out(blocks, dim):
    dims = list(blocks.shape[1:])
    dims[dim] *= blocks.shape[0]
    return jnp.moveaxis(blocks, 0, dim).reshape(dims)


def collect(shard, axis, dim):
    blocks = from_everyone(shard, axis)
    return laid_out(blocks, dim)


def shards(query_slab, eigenbasis, eigenvalues, activations, out_grads):
    highest = lax.Precision.HIGHEST
    slab_here = lax.all_gather(query_slab, "col", axis=0, tiled=True)
    columns = eigenbasis
    share = sent_and_summed(
        lax.dot_general(
            columns,
            slab_here,
            (((0,), (0,)), ((), ())),
            precision=highest,
            preferred_element_type=jnp.float32,
        ),
        "row",
        0,
    )
    scaled_share = share / (eigenvalues + damping)
    columns = eigenbasis
    partial_value = jnp.dot(
        columns,
        collect(scaled_share, "row", 0),
        precision=highest,
        preferred_element_type=jnp.float32,
    )
    preconditioned = sent_and_summed(partial_value, "col", 0)
    projected_part = jnp.dot(
        activations, preconditioned, precision=highest, preferred_element_type=jnp.float32
    )
    projected = lax.psum_scatter(projected_part, ("row", "col"), scatter_dimension=0, tiled=True)
    scores = jnp.sum(projected * out_grads, axis=1)
    return (preconditioned, scores)


def solution(mesh):
    return jax.shard_map(
        shards,
        mesh=mesh,
        in_specs=(
            P(("row", "col"), None),
            P("row", "col"),
            P(("col", "row"), None),
            P(None, ("row", "col")),
            P(("row", "col"), None),
        ),
        out_specs=(P(("row", "col"), None), P(("row", "col"))),
        check_vma=False,
    )
```

profile of v0, /device:TPU:1, one launch (start us, length us, event | category | flops | bytes accessed | tf_op | source)
XLA Modules:
  0.0 411.6 jit_solution(17795620610634855206)
XLA Ops:
  7.2 0.0 copy-start
  7.2 0.0 copy-start.2
  7.2 0.0 all-reduce.3.cloned.1.call-start
  7.2 24.7 %all-gather = f32[8,100,64]{1,2,0:T(8,128)S(1)} all-gather(f32[1,100,64]{1,2,0:T(8,128)} %bitcast.21), channel_id=1, replica_groups=mesh['row'=32,'col'=8] {'col'}, dimensions={0}, use_global_device_ids=true | all-gather | bytes 230400 | tf_op jit(solution)/shard_map/all_gather | solution.py:41
  31.9 0.2 copy.11
  32.1 0.1 reshape.18
  32.2 9.8 %fusion.1 = f32[3200,64]{0,1:T(8,128)S(1)} fusion(f32[800,3200]{1,0:T(8,128)} %param.6, f32[800,64]{0,1:T(8,128)S(1)} %reshape.18), kind=kOutput, calls=%fused_computation.5 | convolution fusion | flops 1966080000 | bytes 11264000 | tf_op jit(solution)/shard_map/dot_general | solution.py:44
  42.0 1.9 reshape.14
  43.9 0.6 copy.12
  44.5 45.2 %all_to_all.15 = f32[32,100,64]{1,2,0:T(8,128)S(1)} all-to-all(f32[32,100,64]{1,2,0:T(8,128)S(1)} %copy.12), channel_id=1, replica_groups=mesh['row'=32,'col'=8] {'row'}, dimensions={0} | all-to-all | bytes 1638400 | tf_op jit(solution)/shard_map/all_to_all | solution.py:17
  89.7 0.1 reduce_sum.27
  89.8 0.0 copy-done.2
  89.8 0.1 broadcast_in_dim.2
  89.9 0.0 copy-start.3
  89.9 33.5 %all_to_all.16 = f32[32,100,64]{1,2,0:T(8,128)S(1)} all-to-all(f32[32,100,64]{1,2,0:T(8,128)S(1)} %broadcast_in_dim.2), channel_id=1, replica_groups=mesh['row'=32,'col'=8] {'row'}, dimensions={0} | all-to-all | bytes 1638400 | tf_op jit(solution)/shard_map/all_to_all | solution.py:23
  123.4 0.6 copy.13
  124.0 0.6 reshape.15
  124.6 16.2 %convolution_bitcast_fusion.1 = f32[800,64]{0,1:T(8,128)S(1)} fusion(f32[3200,64]{0,1:T(8,128)S(1)} %reshape.15, f32[800,3200]{1,0:T(8,128)} %param.6), kind=kOutput, calls=%fused_computation.1 | convolution fusion | flops 1966080000 | bytes 11264000 | tf_op jit(solution)/shard_map/dot_general | solution.py:56
  140.8 0.2 reshape.16
  141.0 0.1 copy.14
  141.0 9.9 %all_to_all.17 = f32[8,100,64]{1,2,0:T(8,128)S(1)} all-to-all(f32[8,100,64]{1,2,0:T(8,128)S(1)} %copy.14), channel_id=1, replica_groups=mesh['row'=32,'col'=8] {'col'}, dimensions={0} | all-to-all | bytes 409600 | tf_op jit(solution)/shard_map/all_to_all | solution.py:17
  151.0 0.0 copy-done
  151.0 0.0 copy-start.1
  151.0 1.4 convolution_bitcast_fusion
  152.4 0.0 all-reduce.3.cloned.1.call-update
  152.5 0.0 copy-done.3
  152.5 0.1 copy.15
  152.6 250.8 %all-reduce.3.cloned.1.call-done = f32[2048,64]{0,1:T(8,128)} async-done(((f32[2048,64]{0,1:T(8,128)}), f32[2048,64]{0,1:T(8,128)}) %all-reduce.3.cloned.1.call-update) | async-done | bytes 524304
  403.4 1.4 fusion
  404.7 0.0 copy-done.1
  (2 shorter events, 0.0 us)
Async XLA Ops:
  7.2 143.8 %copy-start = (f32[2048,100]{0,1:T(8,128)S(1)}, f32[2048,100]{0,1:T(8,128)}, u32[]{:S(2)}) copy-start(f32[2048,100]{0,1:T(8,128)} %param.8) | copy-start | bytes 2457604
  7.2 82.6 %copy-start.2 = (f32[100,64]{0,1:T(8,128)S(1)}, f32[100,64]{0,1:T(8,128)}, u32[]{:S(2)}) copy-start(f32[100,64]{0,1:T(8,128)} %param.7) | copy-start | bytes 76804
  7.2 396.2 %all-reduce.3.cloned.1.call-start = ((), (), s32[]{:S(2)}) async-start(), calls=%async_computation.3 | async-start | bytes 1048576
  89.9 62.6 %copy-start.3 = (f32[8,64]{1,0:T(8,128)S(1)}, f32[8,64]{1,0:T(8,128)}, u32[]{:S(2)}) copy-start(f32[8,64]{1,0:T(8,128)} %param.9) | copy-start | bytes 6148
  151.0 253.7 %copy-start.1 = (f32[100,64]{0,1:T(8,128)}, f32[100,64]{0,1:T(8,128)S(1)}, u32[]{:S(2)}) copy-start(f32[100,64]{0,1:T(8,128)S(1)} %reduce_sum.28) | copy-start | bytes 76804
Sparse Core Ops, SparseCore 0:
  152.6 250.7 all-reduce.2
where the time goes:
time: 413 us; the launch traced here: 412 us
  waiting for transfers between devices  251 us (61%)
  blocking collectives  113 us (27%)
  matrix products  27.3 us (7%)
  between operations  14.2 us (3%)
  local copies, waits for them, and re-layouts  4.46 us (1%)
    unnamed x2, waiting for transfers between devices  251 us
    all_to_all x2, blocking collectives, sent_and_summed(): blocks = lax.all_to_all(in_blocks(shard, dim, size), axis, 0, 0, tiled=True)  55.1 us
    all_to_all x1, blocking collectives, from_everyone(): lax.all_to_all(jnp.broadcast_to(shard[None], (size, *shard.shape)), axis,...  33.5 us
    all_gather x1, blocking collectives, shards(): slab_here = lax.all_gather(query_slab, 'col', axis=0, tiled=True)  24.7 us
    dot_general x1, matrix products, shards(): jnp.dot(columns, collect(scaled_share, 'row', 0), precision=highest, pref...  16.2 us
    dot_general x1, matrix products, shards(): lax.dot_general(columns, slab_here, (((0,), (0,)), ((), ())), precision=h...  9.76 us
  transfers between devices with their start and end apart: 1, of which 1 were waited for; matrix products, arithmetic and copies ran while one was open for 0% of the time, Pallas kernels for 0%

commit v1 on v0

v1 whole, which is shorter than its diff:
```python
import functools

import jax
import jax.numpy as jnp
from jax import lax
from jax.experimental import pallas as pl
from jax.experimental.pallas import tpu as pltpu
from jax.sharding import PartitionSpec as P

damping = 0.1
MESH = pl.DeviceIdType.MESH
f32, bf16 = jnp.float32, jnp.bfloat16
LANES, GROUP = 128, 8
CORES = XH = 2
PIECES = 5


def split(x):
    hi = x.astype(bf16)
    return hi, (x - hi.astype(f32)).astype(bf16)


def stacked(x):
    return jnp.concatenate(split(x), axis=0)


def folded(x):
    half = x.shape[0] // 2
    return x[:half] + x[half:]


def kernel(
    nrow, ncol,
    q_ref, e_ref, v_ref, a_ref, g_ref,
    p_ref, s_ref,
    stage, e_hi, e_lo, q_all, q_cat, x_cat, rot, rot_in, mine, z_in, x_out, x_in,
    v_own, v_all, v_cat, v_use, s_all, s_cat, p_part, p_out, p_in,
    a_own, a_hi, a_lo, g_all, g_own, g_t, f_out, f_in, f_all,
    local, q_sem, g1_sem, v_sem, c_sem, z_sem, x_sem, ag_sem, fw_sem, g2_sem, g3_sem, p_sem, f1_sem, f2_sem,
):
    row, col = lax.axis_index("row"), lax.axis_index("col")
    core, chip = lax.rem(row, CORES), lax.div(row, CORES)
    xh, z = lax.rem(chip, XH), lax.div(chip, XH)
    nchip, nz, nt = nrow // CORES, nrow // (CORES * XH), CORES * ncol
    t = core * ncol + col
    depth, width = e_ref.shape
    r, block = q_ref.shape
    half = rot.shape[2]
    chunks = half // LANES
    pair = 2 * LANES
    partner = (row + 1 - 2 * core, col)
    across = (row + 2 - 4 * xh, col)

    def send(src, dst, sems, i, device):
        return pltpu.make_async_remote_copy(
            src_ref=src, dst_ref=dst, send_sem=sems.at[0, i], recv_sem=sems.at[1, i],
            device_id=device, device_id_type=MESH,
        )

    rows = depth // PIECES
    for i in range(PIECES):
        pltpu.make_async_copy(e_ref.at[pl.ds(i * rows, rows)], stage.at[pl.ds(i * rows, rows)], local.at[i]).start()
    q_copy = pltpu.make_async_copy(q_ref, q_all.at[col], local.at[PIECES])
    g_copy = pltpu.make_async_copy(g_ref, g_all.at[pl.ds(GROUP * t, GROUP)], local.at[PIECES + 1])
    v_copy = pltpu.make_async_copy(v_ref, v_own, local.at[PIECES + 2])
    a_copy = pltpu.make_async_copy(a_ref, a_own, local.at[PIECES + 3])
    q_copy.start()
    g_copy.start()
    v_copy.start()
    a_copy.start()

    barrier = pltpu.get_barrier_semaphore()

    @pl.loop(1, nrow)
    def _(i):
        pl.semaphore_signal(barrier, inc=1, device_id=(lax.rem(row + i, nrow), col), device_id_type=MESH)

    @pl.loop(1, ncol)
    def _(i):
        other = lax.rem(col + i, ncol)
        pl.semaphore_signal(barrier, inc=1, device_id=(row, other), device_id_type=MESH)
        pl.semaphore_signal(barrier, inc=1, device_id=(partner[0], other), device_id_type=MESH)

    def convert(i):
        pltpu.make_async_copy(e_ref.at[pl.ds(i * rows, rows)], stage.at[pl.ds(i * rows, rows)], local.at[i]).wait()

        @pl.loop(0, rows // 16)
        def _(k):
            at = pl.ds(pl.multiple_of(i * rows + k * 16, 16), 16)
            hi, lo = split(stage[at, :])
            e_hi[at, :width] = hi
            e_lo[at, :width] = lo

    pad = jnp.zeros((depth, e_hi.shape[1] - width), bf16)
    e_hi[:, width:] = pad
    e_lo[:, width:] = pad
    v_cat[:, block * nrow:] = jnp.zeros((GROUP, v_cat.shape[1] - block * nrow), f32)
    for i in range(2):
        convert(i)
    q_copy.wait()
    g_copy.wait()
    v_copy.wait()
    pl.semaphore_wait(barrier, nrow - 1 + 2 * (ncol - 1))

    def q_send(i, owner):
        return send(q_all.at[owner], q_all.at[owner], q_sem, i, (row, lax.rem(col + i, ncol)))

    @pl.loop(1, ncol)
    def _(i):
        q_send(i, col).start()

    def g1_send(i, owner):
        to = lax.rem(t + i, nt)
        at = pl.ds(pl.multiple_of(GROUP * owner, GROUP), GROUP)
        return send(g_all.at[at], g_all.at[at], g1_sem, i, (CORES * chip + lax.div(to, ncol), lax.rem(to, ncol)))

    @pl.loop(1, nt)
    def _(i):
        g1_send(i, t).start()

    def v_send(i, owner):
        to = lax.rem(row + i, nrow)
        at = pl.ds(pl.multiple_of(GROUP * lax.div(to, CORES * XH), GROUP), GROUP)
        return send(v_own.at[at], v_all.at[owner], v_sem, i, (to, col))

    @pl.loop(1, nrow)
    def _(i):
        v_send(i, row).start()

    v_all[row] = v_own[pl.ds(pl.multiple_of(GROUP * z, GROUP), GROUP), :]
    for i in range(2, PIECES):
        convert(i)

    @pl.loop(1, ncol)
    def _(i):
        q_send(i, lax.rem(col + ncol - i, ncol)).wait_recv()

    for b in range(ncol):
        q_cat[:, b * block:(b + 1) * block] = q_all[b]
    x_cat[...] = stacked(q_cat[...])

    def rotate(j):
        at = pl.ds(pl.multiple_of(j * pair, pair), pair)
        share = folded(
            jnp.dot(x_cat[...], e_hi[:, at], preferred_element_type=f32)
            + jnp.dot(x_cat[...], e_lo[:, at], preferred_element_type=f32)
        )
        to = pl.ds(pl.multiple_of(j * LANES, LANES), LANES)
        rot[0, :, to] = share[:, :LANES]
        rot[1, :, to] = share[:, LANES:]

    cuts = (0, chunks // 2 + 1, chunks)
    c_copies = []
    for k in range(2):
        pl.loop(cuts[k], cuts[k + 1])(rotate)
        at = pl.ds(cuts[k] * LANES, (cuts[k + 1] - cuts[k]) * LANES)
        c_copies.append(send(rot.at[1 - core, :, at], rot_in.at[:, at], c_sem, k, partner))
        c_copies[k].start()

    @pl.loop(1, nt)
    def _(i):
        g1_send(i, lax.rem(t + nt - i, nt)).wait_recv()

    own_half = pl.ds(pl.multiple_of(core * (r // CORES), r // CORES), r // CORES)
    g_own[...] = g_all[...].T
    g_t[z, xh, own_half] = g_own[own_half, :]

    def g2_send(i, owner):
        part = g_t.at[owner, xh, own_half]
        return send(part, part, g2_sem, i, (CORES * XH * lax.rem(z + i, nz) + CORES * xh + core, col))

    @pl.loop(1, nz)
    def _(i):
        g2_send(i, z).start()

    for copy in c_copies:
        copy.wait_recv()

    @pl.loop(0, nz)
    def _(i):
        at = pl.ds(pl.multiple_of(i * GROUP, GROUP), GROUP)
        mine[at, :] = rot[core, at, :] + rot_in[at, :]

    def z_peer(i):
        return (CORES * XH * lax.rem(z + i, nz) + CORES * xh + core, col)

    def z_send(i, owner):
        at = pl.ds(pl.multiple_of(GROUP * lax.rem(z + i, nz), GROUP), GROUP)
        return send(mine.at[at], z_in.at[owner], z_sem, i, z_peer(i))

    @pl.loop(1, nz)
    def _(i):
        z_send(i, z).start()

    @pl.loop(1, nrow)
    def _(i):
        v_send(i, lax.rem(row + nrow - i, nrow)).wait_recv()

    for b in range(nrow):
        v_cat[:, b * block:(b + 1) * block] = v_all[b]
    for j in range(2 * chunks):
        v_use[j % 2, :, (j // 2) * LANES:(j // 2 + 1) * LANES] = v_cat[:, j * LANES:(j + 1) * LANES]

    a_copy.wait()
    hi, lo = split(a_own[...])
    a_hi[...] = hi
    a_lo[...] = lo

    own_rows = pl.ds(pl.multiple_of(GROUP * z, GROUP), GROUP)

    def z_take(i, total):
        owner = lax.rem(z + nz - i, nz)
        z_send(i, owner).wait_recv()
        return total + z_in[owner]

    x_out[...] = lax.fori_loop(1, nz, z_take, mine[own_rows, :])
    x_copy = send(x_out, x_in, x_sem, 0, across)
    x_copy.start()
    x_copy.wait_recv()
    s_all[core, own_rows, :] = (x_out[...] + x_in[...]) / (v_use[core] + damping)

    def ag_send(i, owner):
        part = s_all.at[core, pl.ds(pl.multiple_of(GROUP * owner, GROUP), GROUP)]
        return send(part, part, ag_sem, i, z_peer(i))

    def fw_send(i, owner, side):
        part = s_all.at[side, pl.ds(pl.multiple_of(GROUP * owner, GROUP), GROUP)]
        return send(part, part, fw_sem, i, partner)

    @pl.loop(1, nz)
    def _(i):
        ag_send(i, z).start()

    fw_send(0, z, core).start()

    @pl.loop(1, nz)
    def _(i):
        g2_send(i, lax.rem(z + nz - i, nz)).wait_recv()

    def g3_send(side):
        part = g_t.at[:, side, own_half]
        return send(part, part, g3_sem, 0, across)

    g3_send(xh).start()

    @pl.loop(1, nz)
    def _(i):
        owner = lax.rem(z + nz - i, nz)
        ag_send(i, owner).wait_recv()
        fw_send(i, owner, core).start()

    g3_send(1 - xh).wait_recv()

    def g4_send(side):
        part = g_t.at[:, :, pl.ds(pl.multiple_of(side * (r // CORES), r // CORES), r // CORES)]
        return send(part, part, g3_sem, 1, partner)

    g4_send(core).start()

    @pl.loop(0, nz)
    def _(i):
        fw_send(i, lax.rem(z + nz - i, nz), 1 - core).wait_recv()

    for j in range(2 * chunks):
        s_cat[:, j * LANES:(j + 1) * LANES] = stacked(s_all[j % 2, :, (j // 2) * LANES:(j // 2 + 1) * LANES])
    over = (((1,), (1,)), ((), ()))
    p_part[...] = folded(
        lax.dot_general(s_cat[...], e_hi[...], over, preferred_element_type=f32)
        + lax.dot_general(s_cat[...], e_lo[...], over, preferred_element_type=f32)
    )
    for b in range(ncol):
        p_out[b] = p_part[:, b * block:(b + 1) * block]

    def p_send(i, owner):
        to = lax.rem(col + i, ncol)
        return send(p_out.at[to], p_in.at[owner], p_sem, i, (row, to))

    @pl.loop(1, ncol)
    def _(i):
        p_send(i, col).start()

    g4_send(1 - core).wait_recv()

    def p_take(i, total):
        owner = lax.rem(col + ncol - i, ncol)
        p_send(i, owner).wait_recv()
        return total + p_in[owner]

    whole = lax.fori_loop(1, ncol, p_take, p_out[col])
    p_ref[...] = whole

    x = stacked(whole)
    for k in range(nchip // 2):
        at = slice(k * pair, (k + 1) * pair)
        projected = folded(
            jnp.dot(x, a_hi[:, at], preferred_element_type=f32) + jnp.dot(x, a_lo[:, at], preferred_element_type=f32)
        )
        for side in range(2):
            there = 2 * k + side
            part = projected[:, side * LANES:(side + 1) * LANES] * g_t[there // XH, there % XH]
            f_out[there] = jnp.sum(part, axis=0, keepdims=True)

    def f1_send(i, owner):
        to = lax.rem(chip + i, nchip)
        return send(f_out.at[to], f_in.at[owner], f1_sem, i, (CORES * to + core, col))

    @pl.loop(1, nchip)
    def _(i):
        f1_send(i, chip).start()

    def f1_take(i, total):
        owner = lax.rem(chip + nchip - i, nchip)
        f1_send(i, owner).wait_recv()
        return total + f_in[owner]

    f_all[t] = lax.fori_loop(1, nchip, f1_take, f_out[chip])

    def f2_send(i, owner):
        to = lax.rem(t + i, nt)
        return send(f_all.at[owner], f_all.at[owner], f2_sem, i, (CORES * chip + lax.div(to, ncol), lax.rem(to, ncol)))

    @pl.loop(1, nt)
    def _(i):
        f2_send(i, t).start()

    def f2_take(i, total):
        owner = lax.rem(t + nt - i, nt)
        f2_send(i, owner).wait_recv()
        return total + f_all[owner]

    total = lax.fori_loop(1, nt, f2_take, f_all[t])
    total = jnp.broadcast_to(total, (GROUP, LANES))
    s_ref[...] = pltpu.roll(total, lax.rem(LANES - GROUP * t, LANES), axis=1)

    @pl.loop(1, ncol)
    def _(i):
        q_send(i, col).wait_send()
        p_send(i, col).wait_send()

    @pl.loop(1, nt)
    def _(i):
        g1_send(i, t).wait_send()
        f2_send(i, t).wait_send()

    @pl.loop(1, nrow)
    def _(i):
        v_send(i, row).wait_send()

    @pl.loop(1, nchip)
    def _(i):
        f1_send(i, chip).wait_send()

    @pl.loop(1, nz)
    def _(i):
        g2_send(i, z).wait_send()
        z_send(i, z).wait_send()
        ag_send(i, z).wait_send()
        fw_send(i, lax.rem(z + nz - i, nz), core).wait_send()

    fw_send(0, z, core).wait_send()
    for copy in c_copies:
        copy.wait_send()
    x_copy.wait_send()
    g3_send(xh).wait_send()
    g4_send(core).wait_send()


def shards(nrow, ncol, query_slab, eigenbasis, eigenvalues, activations, out_grads):
    depth, width = eigenbasis.shape
    block, r = query_slab.shape
    ntrain = activations.shape[0]
    nchip, nz, nt = nrow // CORES, nrow // (CORES * XH), CORES * ncol
    wide = pl.cdiv(width, 2 * LANES) * 2 * LANES
    half = wide // 2
    v, dma = pltpu.VMEM, pltpu.SemaphoreType.DMA
    anywhere = pl.BlockSpec(memory_space=pl.ANY)
    vmem = pl.BlockSpec(memory_space=pltpu.VMEM)
    scratch = [
        v((depth, width), f32), v((depth, wide), bf16), v((depth, wide), bf16),
        v((ncol, r, block), f32), v((r, depth), f32), v((2 * r, depth), bf16),
        v((2, r, half), f32), v((r, half), f32), v((r, half), f32),
        v((nz, GROUP, half), f32), v((GROUP, half), f32), v((GROUP, half), f32),
        v((r, block), f32), v((nrow, GROUP, block), f32), v((GROUP, wide), f32), v((2, GROUP, half), f32),
        v((2, r, half), f32), v((2 * r, wide), bf16),
        v((r, depth), f32), v((ncol, r, block), f32), v((ncol, r, block), f32),
        v((block, ntrain), f32), v((block, ntrain), bf16), v((block, ntrain), bf16),
        v((GROUP * nt, r), f32), v((r, LANES), f32), v((nz, XH, r, LANES), f32),
        v((nchip, 1, LANES), f32), v((nchip, 1, LANES), f32), v((nt, 1, LANES), f32),
        dma((PIECES + 4,)), dma((2, ncol)), dma((2, nt)), dma((2, nrow)), dma((2, 2)), dma((2, nz)), dma((2, 1)),
        dma((2, nz)), dma((2, nz)), dma((2, nz)), dma((2, 2)), dma((2, ncol)), dma((2, nchip)), dma((2, nt)),
    ]
    preconditioned, scores = pl.pallas_call(
        functools.partial(kernel, nrow, ncol),
        out_shape=(jax.ShapeDtypeStruct((r, block), f32), jax.ShapeDtypeStruct((GROUP, LANES), f32)),
        in_specs=[anywhere] * 5,
        out_specs=(vmem, vmem),
        scratch_shapes=scratch,
        compiler_params=pltpu.CompilerParams(collective_id=0, has_side_effects=True, vmem_limit_bytes=60 * 2**20),
    )(query_slab.T, eigenbasis, eigenvalues.T, activations.T, out_grads)
    return preconditioned.T, scores[0, :GROUP]


def solution(mesh):
    return jax.shard_map(
        functools.partial(shards, mesh.shape["row"], mesh.shape["col"]),
        mesh=mesh,
        in_specs=(
            P(("row", "col"), None),
            P("row", "col"),
            P(("col", "row"), None),
            P(None, ("row", "col")),
            P(("row", "col"), None),
        ),
        out_specs=(P(("row", "col"), None), P(("row", "col"))),
        check_vma=False,
    )
```

time: 413 us -> 79 us (0.19)
  waiting for transfers between devices: 251 us -> 0 us
  blocking collectives: 113 us -> 0 us
  Pallas kernels: 0 us -> 75.6 us
  matrix products: 27.3 us -> 0 us
  between operations: 14.2 us -> 0.64 us
    unnamed x2 -> x0, waiting for transfers between devices: 251 us -> none
    all_to_all x3 -> x0, blocking collectives: 88.6 us -> none  [the longest x2 55.1 us: sent_and_summed(): blocks = lax.all_to_all(in_blocks(shard, dim, size), axis, 0, 0, tiled=True)]
    pallas_call x0 -> x1, Pallas kernels: none -> 75.6 us  [shards(): pl.pallas_call(functools.partial(kernel, nrow, ncol), out_shape=(jax.Shap...]
    dot_general x3 -> x0, matrix products: 27.3 us -> none  [the longest x1 16.2 us: shards(): jnp.dot(columns, collect(scaled_share, 'row', 0), precision=highest, pref...]
    all_gather x1 -> x0, blocking collectives: 24.7 us -> none  [shards(): slab_here = lax.all_gather(query_slab, 'col', axis=0, tiled=True)]
  transfers between devices with their start and end apart: 1 -> 0, of which waited for: 1 -> 0; matrix products, arithmetic and copies ran while one was open for 0% -> 0% of each run, Pallas kernels for 0% -> 0%
where the time goes in v1:
time: 79 us; the launch traced here: 78.8 us
  Pallas kernels  75.6 us (96%)
  local copies, waits for them, and re-layouts  2.57 us (3%)
    pallas_call x1, Pallas kernels, shards(): pl.pallas_call(functools.partial(kernel, nrow, ncol), out_shape=(jax.Shap...  75.6 us

profile of v1, /device:TPU:1, one launch (start us, length us, event | category | flops | bytes accessed | tf_op | source)
XLA Modules:
  0.0 78.8 jit_solution(11730330310846290999)
XLA Ops:
  0.6 75.6 %shard_map.68 = (f32[64,100]{1,0:T(8,128)}, f32[8,128]{1,0:T(8,128)}) custom-call(f32[64,100]{1,0:T(8,128)} %bitcast.7, f32[800,3200]{1,0:T(8,128)} %e_ref.1, f32[64,100]{1,0:T(8,128)} %bitcast.8, f32[100,2048]{1,0:T(8,128)} %bitcast.6, f32[8,64]{1,0:T(8,128)} %g_ref.1), custom_call_target="tpu_custom_call" | custom-call | tf_op jit(solution)/shard_map/pallas_call | solution.py:392
  76.3 1.2 %slice_bitcast_fusion = f32[8]{0:T(128)} fusion(f32[8,128]{1,0:T(8,128)} %get-tuple-element.5), kind=kLoop, calls=%fused_computation | loop fusion | bytes 64 | tf_op jit(solution)/shard_map/squeeze | solution.py:400
  77.5 1.4 %copy.8 = f32[100,64]{0,1:T(8,128)} copy(f32[100,64]{0,1:T(8,128)} %bitcast.9) | data formatting | bytes 51200

commit v2 on v0

v2 whole, which is shorter than its diff:
```python
import functools

import jax
import jax.numpy as jnp
from jax import lax
from jax.experimental import pallas as pl
from jax.experimental.pallas import tpu as pltpu
from jax.sharding import PartitionSpec as P

damping = 0.1
MESH = pl.DeviceIdType.MESH
f32, bf16 = jnp.float32, jnp.bfloat16
LANES, GROUP = 128, 8
CORES = XH = 2
XL = 2


def split(x):
    hi = x.astype(bf16)
    return hi, (x - hi.astype(f32)).astype(bf16)


def stacked(x):
    return jnp.concatenate(split(x), axis=0)


def folded(x):
    half = x.shape[0] // 2
    return x[:half] + x[half:]


def kernel(
    nrow, ncol,
    q_ref, e_ref, v_ref, a_ref, g_ref,
    p_ref, s_ref,
    stage, e_hi, e_lo, t_hi, t_lo, q_all, q_cat, x_cat, rot, rot_in, mine, z_in, x_out, x_in,
    v_own, v_all, v_cat, v_use, s_all, s_cat, p_out, p_in, p_own, s_own,
    a_own, a_hi, a_lo, g_all, g_own, g_t, f_out, f_in, f_all,
    e_sem, local, one_sem, q_sem, c_sem, ag_sem,
):
    row, col = lax.axis_index("row"), lax.axis_index("col")
    core, chip = lax.rem(row, CORES), lax.div(row, CORES)
    xh, z = lax.rem(chip, XH), lax.div(chip, XH)
    xl, y = lax.rem(col, XL), lax.div(col, XL)
    nchip, nz, ny, nt = nrow // CORES, nrow // (CORES * XH), ncol // XL, CORES * ncol
    t = core * ncol + col
    depth, width = e_ref.shape
    r, block = q_ref.shape
    half = rot.shape[2]
    chunks = half // LANES
    pair = 2 * LANES
    rows = depth // ny
    partner = (row + 1 - 2 * core, col)
    across = (row + 2 - 4 * xh, col)
    near = sorted(range(ny), key=lambda d: min(d, ny - d))
    Q, G1, V, Z, X, AG, FW, G2, G3, G4, P_, F1, F2 = range(13)

    def send(src, dst, kind, device, recv=None):
        return pltpu.make_async_remote_copy(
            src_ref=src, dst_ref=dst, send_sem=one_sem.at[0, kind], recv_sem=one_sem.at[1, kind] if recv is None else recv,
            device_id=device, device_id_type=MESH,
        )

    def all_in(ref, kind):
        send(ref, ref, kind, partner).wait_recv()

    def all_out(ref, kind):
        send(ref, ref, kind, partner).wait_send()

    def ring(place, i, n):
        return lax.rem(place + i, n)

    def eight(k):
        return pl.ds(pl.multiple_of(GROUP * k, GROUP), GROUP)

    def e_copy(i):
        at = pl.ds(pl.multiple_of(rows * ring(y, near[i], ny), GROUP), rows)
        return pltpu.make_async_copy(e_ref.at[at], stage.at[i], e_sem.at[i])

    q_copy = pltpu.make_async_copy(q_ref, q_all.at[col], local.at[0])
    g_copy = pltpu.make_async_copy(g_ref, g_all.at[eight(t)], local.at[1])
    v_copy = pltpu.make_async_copy(v_ref, v_own, local.at[2])
    a_copy = pltpu.make_async_copy(a_ref, a_own, local.at[3])
    q_copy.start()
    g_copy.start()
    v_copy.start()
    for i in range(ny):
        e_copy(i).start()
    a_copy.start()

    barrier = pltpu.get_barrier_semaphore()

    @pl.loop(1, nrow)
    def _(i):
        pl.semaphore_signal(barrier, inc=1, device_id=(ring(row, i, nrow), col), device_id_type=MESH)

    @pl.loop(1, ncol)
    def _(i):
        other = ring(col, i, ncol)
        pl.semaphore_signal(barrier, inc=1, device_id=(row, other), device_id_type=MESH)
        pl.semaphore_signal(barrier, inc=1, device_id=(partner[0], other), device_id_type=MESH)

    def convert(i):
        e_copy(i).wait()

        def put(at, x):
            hi, lo = split(x)
            e_hi[i, at, :width] = hi
            e_lo[i, at, :width] = lo

        @pl.loop(0, rows // 16)
        def _(k):
            at = pl.ds(pl.multiple_of(k * 16, 16), 16)
            put(at, stage[i, at, :])

        done = rows // 16 * 16
        left = jnp.concatenate([stage[i, done:, :], jnp.zeros((e_hi.shape[1] - rows, width), f32)], axis=0)
        put(slice(done, None), left)

    pad = jnp.zeros((e_hi.shape[1], e_hi.shape[2] - width), bf16)
    for i in range(ny):
        e_hi[i, :, width:] = pad
        e_lo[i, :, width:] = pad
    q_cat[:, XL * block:] = jnp.zeros((r, q_cat.shape[1] - XL * block), f32)
    v_cat[:, block * nrow:] = jnp.zeros((GROUP, v_cat.shape[1] - block * nrow), f32)
    for i in range(2):
        convert(i)
    q_copy.wait()
    g_copy.wait()
    v_copy.wait()
    pl.semaphore_wait(barrier, nrow - 1 + 2 * (ncol - 1))

    own_q = q_all.at[col]
    send(own_q, own_q, Q, (row, col + 1 - 2 * xl), q_sem.at[0]).start()
    for d in near[1:]:
        slot = near.index(ny - d)
        for side in range(XL):
            send(own_q, own_q, Q, (row, XL * ring(y, d, ny) + side), q_sem.at[slot]).start()

    @pl.loop(1, nt)
    def _(i):
        to = ring(t, i, nt)
        part = g_all.at[eight(t)]
        send(part, part, G1, (CORES * chip + lax.div(to, ncol), lax.rem(to, ncol))).start()

    @pl.loop(1, nrow)
    def _(i):
        to = ring(row, i, nrow)
        send(v_own.at[eight(lax.div(to, CORES * XH))], v_all.at[row], V, (to, col)).start()

    v_all[row] = v_own[eight(z), :]
    for i in range(2, ny):
        convert(i)

    def rotate(i, first, last):
        at = pl.ds(first * pair, (last - first) * pair)
        share = folded(
            jnp.dot(x_cat[i], e_hi[i, :, at], preferred_element_type=f32)
            + jnp.dot(x_cat[i], e_lo[i, :, at], preferred_element_type=f32)
        )
        for j in range(first, last):
            for side in range(2):
                k = 2 * (j - first) + side
                part = share[:, k * LANES:(k + 1) * LANES]
                to = pl.ds(j * LANES, LANES)
                if i == 0:
                    rot[side, :, to] = part
                else:
                    rot[side, :, to] += part

    cuts = (0, chunks // 2 + 1, chunks)
    c_copies = []
    own_half = pl.ds(pl.multiple_of(core * (r // CORES), r // CORES), r // CORES)
    for i in range(ny):
        place = ring(y, near[i], ny)
        if i == 0:
            there = q_all.at[pl.ds(XL * place + 1 - xl, 1)]
        else:
            there = q_all.at[pl.ds(XL * place, XL)]
        send(there, there, Q, partner, q_sem.at[i]).wait_recv()
        for side in range(XL):
            q_cat[:, side * block:(side + 1) * block] = q_all[XL * place + side]
        x_cat[i] = stacked(q_cat[...])
        if i == ny - 1:
            all_in(g_all.at[pl.ds(0, GROUP * (nt - 1))], G1)
            g_own[...] = g_all[...].T
            g_t[z, xh, own_half] = g_own[own_half, :]

            @pl.loop(1, nz)
            def _(k):
                part = g_t.at[z, xh, own_half]
                send(part, part, G2, (CORES * XH * ring(z, k, nz) + CORES * xh + core, col)).start()

        for k in range(2):
            rotate(i, cuts[k], cuts[k + 1])
            if i == ny - 1:
                at = pl.ds(cuts[k] * LANES, (cuts[k + 1] - cuts[k]) * LANES)
                c_copies.append(
                    pltpu.make_async_remote_copy(
                        src_ref=rot.at[1 - core, :, at], dst_ref=rot_in.at[:, at], send_sem=c_sem.at[0, k],
                        recv_sem=c_sem.at[1, k], device_id=partner, device_id_type=MESH,
                    )
                )
                c_copies[k].start()

    for copy in c_copies:
        copy.wait_recv()

    @pl.loop(0, nz)
    def _(i):
        mine[eight(i), :] = rot[core, eight(i), :] + rot_in[eight(i), :]

    def z_peer(i):
        return (CORES * XH * ring(z, i, nz) + CORES * xh + core, col)

    @pl.loop(1, nz)
    def _(i):
        send(mine.at[eight(ring(z, i, nz))], z_in.at[z], Z, z_peer(i)).start()

    all_in(v_all.at[pl.ds(0, nrow - 1)], V)
    for b in range(nrow):
        v_cat[:, b * block:(b + 1) * block] = v_all[b]
    for j in range(2 * chunks):
        v_use[j % 2, :, (j // 2) * LANES:(j // 2 + 1) * LANES] = v_cat[:, j * LANES:(j + 1) * LANES]

    all_out(q_all.at[pl.ds(0, ncol - 1)], Q)
    all_out(g_all.at[pl.ds(0, GROUP * (nt - 1))], G1)
    all_out(v_all.at[pl.ds(0, nrow - 1)], V)
    for copy in c_copies:
        copy.wait_send()
    a_copy.wait()
    hi, lo = split(a_own[...])
    a_hi[...] = hi
    a_lo[...] = lo

    @pl.loop(0, chunks)
    def _(j):
        at = pl.ds(pl.multiple_of(j * pair, pair), pair)
        for i in range(ny):
            t_hi[i, at, :] = e_hi[i, :, at].T
            t_lo[i, at, :] = e_lo[i, :, at].T

    all_in(z_in.at[pl.ds(0, nz - 1)], Z)
    x_out[...] = lax.fori_loop(1, nz, lambda i, total: total + z_in[ring(z, i, nz)], mine[eight(z), :])
    send(x_out, x_in, X, across).start()
    all_out(mine.at[pl.ds(0, GROUP * (nz - 1))], Z)
    all_in(x_in, X)
    s_all[core, eight(z), :] = (x_out[...] + x_in[...]) / (v_use[core] + damping)

    def ag_send(i, owner):
        part = s_all.at[core, eight(owner)]
        return send(part, part, AG, z_peer(i), ag_sem.at[i])

    def fw_send(owner):
        part = s_all.at[core, eight(owner)]
        return send(part, part, FW, partner)

    @pl.loop(1, nz)
    def _(i):
        ag_send(i, z).start()

    fw_send(z).start()

    all_out(x_out, X)
    all_in(g_t.at[pl.ds(0, nz - 1), xh, own_half], G2)
    part = g_t.at[:, xh, own_half]
    send(part, part, G3, across).start()

    @pl.loop(1, nz)
    def _(i):
        owner = ring(z, nz - i, nz)
        ag_send(i, owner).wait_recv()
        fw_send(owner).start()

    all_in(g_t.at[:, 1 - xh, own_half], G3)
    part = g_t.at[:, :, own_half]
    send(part, part, G4, partner).start()

    all_in(s_all.at[1 - core], FW)

    for j in range(2 * chunks):
        s_cat[:, j * LANES:(j + 1) * LANES] = stacked(s_all[j % 2, :, (j // 2) * LANES:(j // 2 + 1) * LANES])
    for i in reversed(range(ny)):
        part = folded(
            jnp.dot(s_cat[...], t_hi[i], preferred_element_type=f32)
            + jnp.dot(s_cat[...], t_lo[i], preferred_element_type=f32)
        )
        place = ring(y, near[i], ny)
        for side in range(XL):
            p_out[i, side] = part[:, side * block:(side + 1) * block]
        if i == 0:
            send(p_out.at[0, 1 - xl], p_in.at[col], P_, (row, col + 1 - 2 * xl)).start()
        else:
            for side in range(XL):
                send(p_out.at[i, side], p_in.at[col], P_, (row, XL * place + side)).start()

    all_in(g_t.at[:, :, pl.ds(pl.multiple_of((1 - core) * (r // CORES), r // CORES), r // CORES)], G4)
    all_out(g_t.at[pl.ds(0, nz - 1), xh, own_half], G2)
    all_out(s_all.at[core, pl.ds(0, GROUP * (nz - 1))], AG)
    all_out(s_all.at[core], FW)
    all_out(g_t.at[:, xh, own_half], G3)
    all_out(g_t.at[:, :, own_half], G4)

    all_in(p_in.at[pl.ds(0, ncol - 1)], P_)
    whole = lax.fori_loop(1, ncol, lambda i, total: total + p_in[ring(col, i, ncol)], p_out[0, xl])
    p_own[...] = whole
    p_copy = pltpu.make_async_copy(p_own, p_ref, local.at[0])
    p_copy.start()

    x = stacked(whole)
    for k in range(nchip // 2):
        at = slice(k * pair, (k + 1) * pair)
        projected = folded(
            jnp.dot(x, a_hi[:, at], preferred_element_type=f32) + jnp.dot(x, a_lo[:, at], preferred_element_type=f32)
        )
        for side in range(2):
            there = 2 * k + side
            part = projected[:, side * LANES:(side + 1) * LANES] * g_t[there // XH, there % XH]
            f_out[there] = jnp.sum(part, axis=0, keepdims=True)

    @pl.loop(1, nchip)
    def _(i):
        to = ring(chip, i, nchip)
        send(f_out.at[to], f_in.at[chip], F1, (CORES * to + core, col)).start()

    all_out(p_out.at[0, pl.ds(0, 1)], P_)
    all_out(p_out.at[pl.ds(0, ny - 1)], P_)
    all_in(f_in.at[pl.ds(0, nchip - 1)], F1)
    f_all[t] = lax.fori_loop(1, nchip, lambda i, total: total + f_in[ring(chip, i, nchip)], f_out[chip])

    @pl.loop(1, nt)
    def _(i):
        to = ring(t, i, nt)
        send(f_all.at[t], f_all.at[t], F2, (CORES * chip + lax.div(to, ncol), lax.rem(to, ncol))).start()

    all_out(f_out.at[pl.ds(0, nchip - 1)], F1)
    all_in(f_all.at[pl.ds(0, nt - 1)], F2)
    total = lax.fori_loop(1, nt, lambda i, total: total + f_all[i], f_all[0])
    total = jnp.broadcast_to(total, (GROUP, LANES))
    s_own[...] = pltpu.roll(total, lax.rem(LANES - GROUP * t, LANES), axis=1)
    s_copy = pltpu.make_async_copy(s_own, s_ref, local.at[1])
    s_copy.start()
    all_out(f_all.at[pl.ds(0, nt - 1)], F2)
    p_copy.wait()
    s_copy.wait()


def shards(nrow, ncol, query_slab, eigenbasis, eigenvalues, activations, out_grads):
    depth, width = eigenbasis.shape
    block, r = query_slab.shape
    ntrain = activations.shape[0]
    nchip, nz, ny, nt = nrow // CORES, nrow // (CORES * XH), ncol // XL, CORES * ncol
    wide = pl.cdiv(width, 2 * LANES) * 2 * LANES
    half = wide // 2
    rows = depth // ny
    deep = pl.cdiv(rows, 16) * 16
    v, dma = pltpu.VMEM, pltpu.SemaphoreType.DMA
    anywhere = pl.BlockSpec(memory_space=pl.ANY)
    scratch = [
        v((ny, rows, width), f32), v((ny, deep, wide), bf16), v((ny, deep, wide), bf16),
        v((ny, wide, deep), bf16), v((ny, wide, deep), bf16),
        v((ncol, r, block), f32), v((r, deep), f32), v((ny, 2 * r, deep), bf16),
        v((2, r, half), f32), v((r, half), f32), v((r, half), f32),
        v((nz, GROUP, half), f32), v((GROUP, half), f32), v((GROUP, half), f32),
        v((r, block), f32), v((nrow, GROUP, block), f32), v((GROUP, wide), f32), v((2, GROUP, half), f32),
        v((2, r, half), f32), v((2 * r, wide), bf16),
        v((ny, XL, r, block), f32), v((ncol, r, block), f32), v((r, block), f32), v((GROUP, LANES), f32),
        v((block, ntrain), f32), v((block, ntrain), bf16), v((block, ntrain), bf16),
        v((GROUP * nt, r), f32), v((r, LANES), f32), v((nz, XH, r, LANES), f32),
        v((nchip, 1, LANES), f32), v((nchip, 1, LANES), f32), v((nt, 1, LANES), f32),
        dma((ny,)), dma((4,)), dma((2, 13)), dma((ny,)), dma((2, 2)), dma((nz,)),
    ]
    preconditioned, scores = pl.pallas_call(
        functools.partial(kernel, nrow, ncol),
        out_shape=(jax.ShapeDtypeStruct((r, block), f32), jax.ShapeDtypeStruct((GROUP, LANES), f32)),
        in_specs=[anywhere] * 5,
        out_specs=(anywhere, anywhere),
        scratch_shapes=scratch,
        compiler_params=pltpu.CompilerParams(collective_id=0, has_side_effects=True, vmem_limit_bytes=60 * 2**20),
    )(query_slab.T, eigenbasis, eigenvalues.T, activations.T, out_grads)
    return preconditioned.T, scores[0, :GROUP]


def solution(mesh):
    return jax.shard_map(
        functools.partial(shards, mesh.shape["row"], mesh.shape["col"]),
        mesh=mesh,
        in_specs=(
            P(("row", "col"), None),
            P("row", "col"),
            P(("col", "row"), None),
            P(None, ("row", "col")),
            P(("row", "col"), None),
        ),
        out_specs=(P(("row", "col"), None), P(("row", "col"))),
        check_vma=False,
    )
```

time: 413 us -> 71.8 us (0.17)
  waiting for transfers between devices: 251 us -> 0 us
  blocking collectives: 113 us -> 0 us
  Pallas kernels: 0 us -> 68.4 us
  matrix products: 27.3 us -> 0 us
  between operations: 14.2 us -> 0.64 us
    unnamed x2 -> x0, waiting for transfers between devices: 251 us -> none
    all_to_all x3 -> x0, blocking collectives: 88.6 us -> none  [the longest x2 55.1 us: sent_and_summed(): blocks = lax.all_to_all(in_blocks(shard, dim, size), axis, 0, 0, tiled=True)]
    pallas_call x0 -> x1, Pallas kernels: none -> 68.4 us  [shards(): pl.pallas_call(functools.partial(kernel, nrow, ncol), out_shape=(jax.Shap...]
    dot_general x3 -> x0, matrix products: 27.3 us -> none  [the longest x1 16.2 us: shards(): jnp.dot(columns, collect(scaled_share, 'row', 0), precision=highest, pref...]
    all_gather x1 -> x0, blocking collectives: 24.7 us -> none  [shards(): slab_here = lax.all_gather(query_slab, 'col', axis=0, tiled=True)]
  transfers between devices with their start and end apart: 1 -> 0, of which waited for: 1 -> 0; matrix products, arithmetic and copies ran while one was open for 0% -> 0% of each run, Pallas kernels for 0% -> 0%
where the time goes in v2:
time: 71.8 us; the launch traced here: 71.6 us
  Pallas kernels  68.4 us (95%)
  local copies, waits for them, and re-layouts  2.57 us (4%)
    pallas_call x1, Pallas kernels, shards(): pl.pallas_call(functools.partial(kernel, nrow, ncol), out_shape=(jax.Shap...  68.4 us

profile of v2, /device:TPU:1, one launch (start us, length us, event | category | flops | bytes accessed | tf_op | source)
XLA Modules:
  0.0 71.6 jit_solution(10246050965685315411)
XLA Ops:
  0.6 68.4 %shard_map.68 = (f32[64,100]{1,0:T(8,128)}, f32[8,128]{1,0:T(8,128)}) custom-call(f32[64,100]{1,0:T(8,128)} %bitcast.7, f32[800,3200]{1,0:T(8,128)} %e_ref.1, f32[64,100]{1,0:T(8,128)} %bitcast.8, f32[100,2048]{1,0:T(8,128)} %bitcast.6, f32[8,64]{1,0:T(8,128)} %g_ref.1), custom_call_target="tpu_custom_call" | custom-call | tf_op jit(solution)/shard_map/pallas_call | solution.py:373
  69.1 1.2 %slice_bitcast_fusion = f32[8]{0:T(128)} fusion(f32[8,128]{1,0:T(8,128)} %get-tuple-element.5), kind=kLoop, calls=%fused_computation | loop fusion | bytes 64 | tf_op jit(solution)/shard_map/squeeze | solution.py:381
  70.2 1.4 %copy.8 = f32[100,64]{0,1:T(8,128)} copy(f32[100,64]{0,1:T(8,128)} %bitcast.9) | data formatting | bytes 51200

commit v3 on v2

v3 whole, which is shorter than its diff:
```python
import functools

import jax
import jax.numpy as jnp
from jax import lax
from jax.experimental import pallas as pl
from jax.experimental.pallas import tpu as pltpu
from jax.sharding import PartitionSpec as P

damping = 0.1
MESH = pl.DeviceIdType.MESH
f32, bf16 = jnp.float32, jnp.bfloat16
LANES, GROUP = 128, 8
CORES = XH = 2
XL = 2


def split(x):
    hi = x.astype(bf16)
    return hi, (x - hi.astype(f32)).astype(bf16)


def stacked(x):
    return jnp.concatenate(split(x), axis=0)


def folded(x):
    half = x.shape[0] // 2
    return x[:half] + x[half:]


def kernel(
    nrow, ncol,
    q_ref, e_ref, v_ref, a_ref, g_ref,
    p_ref, s_ref,
    stage, e_hi, e_lo, t_hi, t_lo, q_all, q_cat, x_cat, rot, rot_in, mine, z_far, z_mid, z_out, z_in, x_out, x_in,
    v_own, v_all, v_cat, v_use, s_all, s_cat, p_own, p_out, p_in,
    a_own, a_hi, a_lo, g_all, g_own, g_t, f_out, f_in, f_sum, f_all,
    e_sem, local, one_sem, q_sem, c_sem, z_sem, x_sem, ag_sem,
):
    row, col = lax.axis_index("row"), lax.axis_index("col")
    core, chip = lax.rem(row, CORES), lax.div(row, CORES)
    xh, z = lax.rem(chip, XH), lax.div(chip, XH)
    xl, y = lax.rem(col, XL), lax.div(col, XL)
    nchip, nz, ny, nt = nrow // CORES, nrow // (CORES * XH), ncol // XL, CORES * ncol
    t = core * ncol + col
    depth, width = e_ref.shape
    r, block = q_ref.shape
    half = rot.shape[2]
    chunks = half // LANES
    pair = 2 * LANES
    rows = depth // ny
    partner = (row + 1 - 2 * core, col)
    across = (row + 2 - 4 * xh, col)
    near = sorted(range(ny), key=lambda d: min(d, ny - d))
    Q, G1, V, V2, AG, FW, G2, G3, G4, P_, F1, F2 = range(12)
    corner = XH * xh + core

    def send(src, dst, kind, device, recv=None):
        return pltpu.make_async_remote_copy(
            src_ref=src, dst_ref=dst, send_sem=one_sem.at[0, kind], recv_sem=one_sem.at[1, kind] if recv is None else recv,
            device_id=device, device_id_type=MESH,
        )

    def all_in(ref, kind):
        send(ref, ref, kind, partner).wait_recv()

    def all_out(ref, kind):
        send(ref, ref, kind, partner).wait_send()

    def ring(place, i, n):
        return lax.rem(place + i, n)

    def eight(k):
        return pl.ds(pl.multiple_of(GROUP * k, GROUP), GROUP)

    def e_copy(i):
        at = pl.ds(pl.multiple_of(rows * ring(y, near[i], ny), GROUP), rows)
        return pltpu.make_async_copy(e_ref.at[at], stage.at[i], e_sem.at[i])

    q_copy = pltpu.make_async_copy(q_ref, q_all.at[col], local.at[0])
    g_copy = pltpu.make_async_copy(g_ref, g_all.at[eight(t)], local.at[1])
    v_copy = pltpu.make_async_copy(v_ref, v_own, local.at[2])
    a_copy = pltpu.make_async_copy(a_ref, a_own, local.at[3])
    q_copy.start()
    g_copy.start()
    v_copy.start()
    for i in range(ny):
        e_copy(i).start()
    a_copy.start()

    barrier = pltpu.get_barrier_semaphore()

    @pl.loop(1, nrow)
    def _(i):
        pl.semaphore_signal(barrier, inc=1, device_id=(ring(row, i, nrow), col), device_id_type=MESH)

    @pl.loop(1, ncol)
    def _(i):
        other = ring(col, i, ncol)
        pl.semaphore_signal(barrier, inc=1, device_id=(row, other), device_id_type=MESH)
        pl.semaphore_signal(barrier, inc=1, device_id=(partner[0], other), device_id_type=MESH)

    def convert(i):
        e_copy(i).wait()

        def put(at, x):
            hi, lo = split(x)
            e_hi[i, at, :width] = hi
            e_lo[i, at, :width] = lo

        @pl.loop(0, rows // 16)
        def _(k):
            at = pl.ds(pl.multiple_of(k * 16, 16), 16)
            put(at, stage[i, at, :])

        done = rows // 16 * 16
        left = jnp.concatenate([stage[i, done:, :], jnp.zeros((e_hi.shape[1] - rows, width), f32)], axis=0)
        put(slice(done, None), left)

    q_copy.wait()
    g_copy.wait()
    v_copy.wait()
    pl.semaphore_wait(barrier, nrow - 1 + 2 * (ncol - 1))

    own_q = q_all.at[col]
    send(own_q, own_q, Q, (row, col + 1 - 2 * xl), q_sem.at[0]).start()

    def q_send(places):
        for d in places:
            slot = near.index(ny - d)
            for side in range(XL):
                send(own_q, own_q, Q, (row, XL * ring(y, d, ny) + side), q_sem.at[slot]).start()

    q_send(near[1:-1])

    @pl.loop(1, nt)
    def _(i):
        to = ring(t, i, nt)
        part = g_all.at[eight(t)]
        send(part, part, G1, (CORES * chip + lax.div(to, ncol), lax.rem(to, ncol))).start()

    q_send(near[-1:])

    def z_peer(i):
        return (CORES * XH * ring(z, i, nz) + corner, col)

    @pl.loop(1, nz)
    def _(i):
        send(v_own.at[eight(ring(z, i, nz))], v_all.at[z, corner], V, z_peer(i)).start()

    pad = jnp.zeros((e_hi.shape[1], e_hi.shape[2] - width), bf16)
    for i in range(ny):
        e_hi[i, :, width:] = pad
        e_lo[i, :, width:] = pad
    q_cat[:, XL * block:] = jnp.zeros((r, q_cat.shape[1] - XL * block), f32)
    v_cat[:, block * nrow:] = jnp.zeros((GROUP, v_cat.shape[1] - block * nrow), f32)
    v_all[z, corner] = v_own[eight(z), :]
    for i in range(ny):
        convert(i)

    def rotate(i, first, last):
        at = pl.ds(first * pair, (last - first) * pair)
        share = folded(
            jnp.dot(x_cat[i], e_hi[i, :, at], preferred_element_type=f32)
            + jnp.dot(x_cat[i], e_lo[i, :, at], preferred_element_type=f32)
        )
        for j in range(first, last):
            for side in range(2):
                k = 2 * (j - first) + side
                part = share[:, k * LANES:(k + 1) * LANES]
                to = pl.ds(j * LANES, LANES)
                if i == 0:
                    rot[side, :, to] = part
                else:
                    rot[side, :, to] += part

    cuts = (0, chunks // 2 + 1, chunks)
    c_copies = []
    own_half = pl.ds(pl.multiple_of(core * (r // CORES), r // CORES), r // CORES)
    for i in range(ny):
        if i == ny - 1:
            all_in(v_all.at[pl.ds(0, nz - 1), corner], V)
            part = v_all.at[:, corner]
            for other in (partner, across, (across[0] + 1 - 2 * core, col)):
                send(part, part, V2, other).start()

            all_in(g_all.at[pl.ds(0, GROUP * (nt - 1))], G1)
            g_own[...] = g_all[...].T
            g_t[z, xh, own_half] = g_own[own_half, :]

            @pl.loop(1, nz)
            def _(k):
                part = g_t.at[z, xh, own_half]
                send(part, part, G2, z_peer(k)).start()

        place = ring(y, near[i], ny)
        if i == 0:
            there = q_all.at[pl.ds(XL * place + 1 - xl, 1)]
        else:
            there = q_all.at[pl.ds(XL * place, XL)]
        send(there, there, Q, partner, q_sem.at[i]).wait_recv()
        for side in range(XL):
            q_cat[:, side * block:(side + 1) * block] = q_all[XL * place + side]
        x_cat[i] = stacked(q_cat[...])
        for k in range(2):
            rotate(i, cuts[k], cuts[k + 1])
            if i == ny - 1:
                at = pl.ds(cuts[k] * LANES, (cuts[k + 1] - cuts[k]) * LANES)
                c_copies.append(
                    pltpu.make_async_remote_copy(
                        src_ref=rot.at[1 - core, :, at], dst_ref=rot_in.at[:, at], send_sem=c_sem.at[0, k],
                        recv_sem=c_sem.at[1, k], device_id=partner, device_id_type=MESH,
                    )
                )
                c_copies[k].start()

    lanes, halves = [], []
    for a, b in zip(cuts, cuts[1:]):
        middle = (a + b + 1) // 2
        lanes.append(pl.ds(a * LANES, (b - a) * LANES))
        halves.append((pl.ds(a * LANES, (middle - a) * LANES), pl.ds(middle * LANES, (b - middle) * LANES)))
    ways = ((1, 0), (nz - 1, 1))
    FIRST, MIDDLE, LAST, THROUGH = range(4)

    def z_send(src, dst, sent, landed, k, i):
        return pltpu.make_async_remote_copy(
            src_ref=src, dst_ref=dst, send_sem=z_sem.at[sent, k], recv_sem=z_sem.at[landed, k], device_id=z_peer(i),
            device_id_type=MESH,
        )

    for k, at in enumerate(lanes):
        c_copies[k].wait_recv()

        @pl.loop(0, nz)
        def _(i):
            mine[eight(i), at] = rot[core, eight(i), at] + rot_in[eight(i), at]

        for step, way in ways:
            part = halves[k][way]
            z_send(mine.at[eight(ring(z, nz // 2, nz)), part], z_far.at[way, :, part], FIRST, MIDDLE, k, 2 * step % nz).start()
        for step, way in ways:
            z_send(mine.at[eight(ring(z, 3 * step % nz, nz)), at], z_mid.at[way, :, at], FIRST, MIDDLE, k, step).start()

    for k, at in enumerate(lanes):
        for step, way in ways:
            z_send(mine.at[eight(ring(z, step, nz)), at], z_in.at[way, :, at], FIRST, LAST, k, step).start()

    def through(k):
        at = lanes[k]
        there = z_in.at[pl.ds(0, 3), :, at]
        z_send(there, there, FIRST, MIDDLE, k, 1).wait_recv()
        for step, way in ways:
            z_out[way, :, at] = mine[eight(ring(z, 2 * step % nz, nz)), at] + z_mid[way, :, at]
            z_out[way, :, halves[k][way]] += z_far[way, :, halves[k][way]]
        for step, way in ways:
            z_send(z_out.at[way, :, at], z_in.at[2 + way, :, at], THROUGH, LAST, k, 2 * step % nz).start()

    def transpose(first, last):
        @pl.loop(first, last)
        def _(j):
            at = pl.ds(pl.multiple_of(j * pair, pair), pair)
            to = pl.ds(pl.multiple_of(j * LANES, LANES), LANES)
            for i in range(ny):
                hi, lo = e_hi[i, :, at].T, e_lo[i, :, at].T
                for side in range(2):
                    t_hi[side, i, to, :] = hi[side * LANES:(side + 1) * LANES]
                    t_lo[side, i, to, :] = lo[side * LANES:(side + 1) * LANES]

    transpose(0, chunks * 3 // 4)
    for k in range(2):
        through(k)
    all_in(g_t.at[pl.ds(0, nz - 1), xh, own_half], G2)
    part = g_t.at[:, xh, own_half]
    send(part, part, G3, across).start()
    transpose(chunks * 3 // 4, chunks)

    def x_copy(k):
        at = lanes[k]
        return pltpu.make_async_remote_copy(
            src_ref=x_out.at[:, at], dst_ref=x_in.at[:, at], send_sem=x_sem.at[0, k], recv_sem=x_sem.at[1, k],
            device_id=across, device_id_type=MESH,
        )

    def ag_send(i, owner, at, k, kind):
        part = s_all.at[core, eight(owner), at]
        return send(part, part, AG, z_peer(i), ag_sem.at[k, kind])

    def fw_send(owner, at):
        part = s_all.at[core, eight(owner), at]
        return send(part, part, FW, partner)

    for k, at in enumerate(lanes):
        there = z_in.at[:, :, at]
        z_send(there, there, FIRST, LAST, k, 1).wait_recv()
        x_out[:, at] = mine[eight(z), at] + (z_in[0, :, at] + z_in[1, :, at]) + (z_in[2, :, at] + z_in[3, :, at])
        x_copy(k).start()

    all_in(v_all.at[:, pl.ds(0, CORES * XH - 1)], V2)
    for b in range(nrow):
        v_cat[:, b * block:(b + 1) * block] = v_all[b // (CORES * XH), b % (CORES * XH)]
    for j in range(2 * chunks):
        v_use[j % 2, :, (j // 2) * LANES:(j // 2 + 1) * LANES] = v_cat[:, j * LANES:(j + 1) * LANES]

    all_out(q_all.at[pl.ds(0, ncol - 1)], Q)
    all_out(g_all.at[pl.ds(0, GROUP * (nt - 1))], G1)
    all_out(v_all.at[pl.ds(0, nz - 1), corner], V)
    all_out(v_all.at[:, pl.ds(0, CORES * XH - 1)], V2)
    for copy in c_copies:
        copy.wait_send()
    for k, at in enumerate(lanes):
        there = mine.at[pl.ds(0, 5 * GROUP), at]
        z_send(there, there, FIRST, LAST, k, 1).wait_send()
        there = z_out.at[:, :, at]
        z_send(there, there, THROUGH, LAST, k, 1).wait_send()
    a_copy.wait()
    hi, lo = split(a_own[...])
    a_hi[...] = hi
    a_lo[...] = lo

    for k, at in enumerate(lanes):
        x_copy(k).wait()
        s_all[core, eight(z), at] = (x_out[:, at] + x_in[:, at]) / (v_use[core, :, at] + damping)
        for step, way in ways:
            ag_send(2 * step % nz, z, at, k, 2 + way).start()
        fw_send(z, at).start()

    for k, at in enumerate(lanes):
        for step, way in ways:
            ag_send(step, z, at, k, way).start()

    for k, at in enumerate(lanes):
        for step, way in ways:
            owner = ring(z, nz - 2 * step % nz, nz)
            ag_send(1, owner, at, k, 2 + way).wait_recv()
            ag_send(2 * step % nz, owner, halves[k][way], k, 6 + way).start()
            ag_send(step, owner, at, k, 4 + way).start()
            fw_send(owner, at).start()
        if k == 0:
            all_in(g_t.at[:, 1 - xh, own_half], G3)
            part = g_t.at[:, :, own_half]
            send(part, part, G4, partner).start()

    for k, at in enumerate(lanes):
        for away, kind in ((1, 0), (3, 4)):
            for step, way in ways:
                owner = ring(z, nz - away * step % nz, nz)
                ag_send(1, owner, at, k, kind + way).wait_recv()
                fw_send(owner, at).start()
        for step, way in ways:
            owner = ring(z, nz // 2, nz)
            ag_send(1, owner, halves[k][way], k, 6 + way).wait_recv()
            fw_send(owner, halves[k][way]).start()

    def back(side, i):
        return folded(
            jnp.dot(s_cat[side], t_hi[side, i], preferred_element_type=f32)
            + jnp.dot(s_cat[side], t_lo[side, i], preferred_element_type=f32)
        )

    s_cat[core] = stacked(s_all[core])
    for i in range(ny):
        p_own[i] = back(core, i)
    all_in(s_all.at[1 - core], FW)
    s_cat[1 - core] = stacked(s_all[1 - core])
    for group in ((3, 2), (1, 0)):
        for i in group:
            part = p_own[i] + back(1 - core, i)
            for side in range(XL):
                p_out[i, side] = part[:, side * block:(side + 1) * block]
        for i in group:
            if i == 0:
                send(p_out.at[0, 1 - xl], p_in.at[col], P_, (row, col + 1 - 2 * xl)).start()
            else:
                place = ring(y, near[i], ny)
                for side in range(XL):
                    send(p_out.at[i, side], p_in.at[col], P_, (row, XL * place + side)).start()

    all_in(g_t.at[:, :, pl.ds(pl.multiple_of((1 - core) * (r // CORES), r // CORES), r // CORES)], G4)
    all_out(g_t.at[pl.ds(0, nz - 1), xh, own_half], G2)
    all_out(s_all.at[core, pl.ds(0, GROUP * (nz - 1))], AG)
    all_out(s_all.at[core], FW)
    all_out(g_t.at[:, xh, own_half], G3)
    all_out(g_t.at[:, :, own_half], G4)

    all_in(p_in.at[pl.ds(0, ncol - 1)], P_)
    whole = lax.fori_loop(1, ncol, lambda i, total: total + p_in[ring(col, i, ncol)], p_out[0, xl])
    p_ref[...] = whole

    x = stacked(whole)
    for k in range(nchip // 2):
        at = slice(k * pair, (k + 1) * pair)
        projected = folded(
            jnp.dot(x, a_hi[:, at], preferred_element_type=f32) + jnp.dot(x, a_lo[:, at], preferred_element_type=f32)
        )
        for side in range(2):
            there = 2 * k + side
            part = projected[:, side * LANES:(side + 1) * LANES] * g_t[there // XH, there % XH]
            f_out[there // XH, there % XH] = jnp.sum(part, axis=0, keepdims=True)

    place, nplace = CORES * z + core, CORES * nz

    @pl.loop(1, nplace)
    def _(i):
        to = ring(place, i, nplace)
        there = lax.div(to, CORES)
        send(f_out.at[there], f_in.at[place], F1, (CORES * (XH * there + xh) + lax.rem(to, CORES), col)).start()

    all_out(p_in.at[pl.ds(0, ncol - 1)], P_)
    all_in(f_in.at[pl.ds(0, nplace - 1)], F1)
    f_sum[...] = lax.fori_loop(1, nplace, lambda i, total: total + f_in[ring(place, i, nplace)], f_out[z])

    spot, nspot = ncol * xh + col, XH * ncol

    @pl.loop(1, nspot)
    def _(i):
        to = ring(spot, i, nspot)
        there = lax.div(to, ncol)
        send(f_sum.at[there], f_all.at[spot], F2, (CORES * (XH * z + there) + core, lax.rem(to, ncol))).start()

    all_out(f_in.at[pl.ds(0, nplace - 1)], F1)
    all_in(f_all.at[pl.ds(0, nspot - 1)], F2)
    total = lax.fori_loop(1, nspot, lambda i, total: total + f_all[ring(spot, i, nspot)], f_sum[xh])
    total = jnp.broadcast_to(total, (GROUP, LANES))
    s_ref[...] = pltpu.roll(total, lax.rem(LANES - GROUP * t, LANES), axis=1)
    all_out(f_all.at[pl.ds(0, nspot - 1)], F2)


def shards(nrow, ncol, query_slab, eigenbasis, eigenvalues, activations, out_grads):
    depth, width = eigenbasis.shape
    block, r = query_slab.shape
    ntrain = activations.shape[0]
    nchip, nz, ny, nt = nrow // CORES, nrow // (CORES * XH), ncol // XL, CORES * ncol
    wide = pl.cdiv(width, 2 * LANES) * 2 * LANES
    half = wide // 2
    rows = depth // ny
    deep = pl.cdiv(rows, 16) * 16
    v, dma = pltpu.VMEM, pltpu.SemaphoreType.DMA
    anywhere, vmem = pl.BlockSpec(memory_space=pl.ANY), pl.BlockSpec(memory_space=pltpu.VMEM)
    scratch = [
        v((ny, rows, width), f32), v((ny, deep, wide), bf16), v((ny, deep, wide), bf16),
        v((2, ny, half, deep), bf16), v((2, ny, half, deep), bf16),
        v((ncol, r, block), f32), v((r, deep), f32), v((ny, 2 * r, deep), bf16),
        v((2, r, half), f32), v((r, half), f32), v((r, half), f32),
        v((2, GROUP, half), f32), v((2, GROUP, half), f32), v((2, GROUP, half), f32), v((4, GROUP, half), f32),
        v((GROUP, half), f32), v((GROUP, half), f32),
        v((r, block), f32), v((nz, CORES * XH, GROUP, block), f32), v((GROUP, wide), f32), v((2, GROUP, half), f32),
        v((2, r, half), f32), v((2, 2 * r, half), bf16), v((ny, r, deep), f32),
        v((ny, XL, r, block), f32), v((ncol, r, block), f32),
        v((block, ntrain), f32), v((block, ntrain), bf16), v((block, ntrain), bf16),
        v((GROUP * nt, r), f32), v((r, LANES), f32), v((nz, XH, r, LANES), f32),
        v((nz, XH, 1, LANES), f32), v((CORES * nz, XH, 1, LANES), f32), v((XH, 1, LANES), f32), v((nt, 1, LANES), f32),
        dma((ny,)), dma((4,)), dma((2, 12)), dma((ny,)), dma((2, 2)), dma((4, 2)), dma((2, 2)), dma((2, 8)),
    ]
    preconditioned, scores = pl.pallas_call(
        functools.partial(kernel, nrow, ncol),
        out_shape=(pltpu.VMEM((r, block), f32), pltpu.VMEM((GROUP, LANES), f32)),
        in_specs=[anywhere] * 5,
        out_specs=(vmem, vmem),
        scratch_shapes=scratch,
        compiler_params=pltpu.CompilerParams(collective_id=0, has_side_effects=True, vmem_limit_bytes=60 * 2**20),
    )(query_slab.T, eigenbasis, eigenvalues.T, activations.T, out_grads)
    return preconditioned.T, scores[0, :GROUP]


def solution(mesh):
    return jax.shard_map(
        functools.partial(shards, mesh.shape["row"], mesh.shape["col"]),
        mesh=mesh,
        in_specs=(
            P(("row", "col"), None),
            P("row", "col"),
            P(("col", "row"), None),
            P(None, ("row", "col")),
            P(("row", "col"), None),
        ),
        out_specs=(P(("row", "col"), None), P(("row", "col"))),
        check_vma=False,
    )
```

time: 71.8 us -> 60.9 us (0.85)
  Pallas kernels: 68.4 us -> 59.1 us
  local copies, waits for them, and re-layouts: 2.57 us -> 1.13 us
    pallas_call x1, Pallas kernels: 68.4 us -> 59.1 us  [shards(): pl.pallas_call(functools.partial(kernel, nrow, ncol), out_shape=(pltpu.VM...]
    unnamed x1, local copies, waits for them, and re-layouts: 1.37 us -> 0.62 us
where the time goes in v3:
time: 60.9 us
  Pallas kernels  59.1 us (97%)
  local copies, waits for them, and re-layouts  1.13 us (2%)
  between operations  0.64 us (1%)
    pallas_call x1, Pallas kernels, shards(): pl.pallas_call(functools.partial(kernel, nrow, ncol), out_shape=(pltpu.VM...  59.1 us

profile of v3, /device:TPU:1, one launch (start us, length us, event | category | flops | bytes accessed | tf_op | source)
XLA Modules:
  0.0 60.9 jit_solution(6348850641064512075)
XLA Ops:
  0.6 59.1 %shard_map.68 = (f32[64,100]{1,0:T(8,128)S(1)}, f32[8,128]{1,0:T(8,128)S(1)}) custom-call(f32[64,100]{1,0:T(8,128)} %bitcast.8, f32[800,3200]{1,0:T(8,128)} %e_ref.1, f32[64,100]{1,0:T(8,128)} %bitcast.9, f32[100,2048]{1,0:T(8,128)} %bitcast.7, f32[8,64]{1,0:T(8,128)} %g_ref.1), custom_call_target="tpu_custom_call" | custom-call | tf_op jit(solution)/shard_map/pallas_call | solution.py:455
  59.7 0.6 %copy.8 = f32[100,64]{0,1:T(8,128)} copy(f32[100,64]{0,1:T(8,128)S(1)} %bitcast.6) | data formatting | bytes 51200
  60.3 0.5 slice_bitcast_fusion

commit v4 on v3

--- a/solution.py
+++ b/solution.py
@@ -36,7 +36,7 @@
     stage, e_hi, e_lo, t_hi, t_lo, q_all, q_cat, x_cat, rot, rot_in, mine, z_far, z_mid, z_out, z_in, x_out, x_in,
     v_own, v_all, v_cat, v_use, s_all, s_cat, p_own, p_out, p_in,
     a_own, a_hi, a_lo, g_all, g_own, g_t, f_out, f_in, f_sum, f_all,
-    e_sem, local, one_sem, q_sem, c_sem, z_sem, x_sem, ag_sem,
+    e_sem, local, one_sem, v_sem, q_sem, c_sem, z_sem, x_sem, ag_sem,
 ):
     row, col = lax.axis_index("row"), lax.axis_index("col")
     core, chip = lax.rem(row, CORES), lax.div(row, CORES)
@@ -90,10 +90,12 @@
     a_copy.start()
 
     barrier = pltpu.get_barrier_semaphore()
-
-    @pl.loop(1, nrow)
-    def _(i):
-        pl.semaphore_signal(barrier, inc=1, device_id=(ring(row, i, nrow), col), device_id_type=MESH)
+    diagonal = (across[0] + 1 - 2 * core, col)
+
+    def z_peer(i):
+        return (CORES * XH * ring(z, i, nz) + corner, col)
+
+    close = (1, nz - 1, 2, nz - 2)
 
     @pl.loop(1, ncol)
     def _(i):
@@ -101,6 +103,9 @@
         pl.semaphore_signal(barrier, inc=1, device_id=(row, other), device_id_type=MESH)
         pl.semaphore_signal(barrier, inc=1, device_id=(partner[0], other), device_id_type=MESH)
 
+    for device in (*(z_peer(i) for i in close), across, diagonal, partner):
+        pl.semaphore_signal(barrier, inc=1, device_id=device, device_id_type=MESH)
+
     def convert(i):
         e_copy(i).wait()
 
@@ -121,7 +126,7 @@
     q_copy.wait()
     g_copy.wait()
     v_copy.wait()
-    pl.semaphore_wait(barrier, nrow - 1 + 2 * (ncol - 1))
+    pl.semaphore_wait(barrier, 2 * (ncol - 1) + len(close) + 3)
 
     own_q = q_all.at[col]
     send(own_q, own_q, Q, (row, col + 1 - 2 * xl), q_sem.at[0]).start()
@@ -142,12 +147,14 @@
 
     q_send(near[-1:])
 
-    def z_peer(i):
-        return (CORES * XH * ring(z, i, nz) + corner, col)
-
-    @pl.loop(1, nz)
-    def _(i):
-        send(v_own.at[eight(ring(z, i, nz))], v_all.at[z, corner], V, z_peer(i)).start()
+    def v_send(i, owner):
+        return send(v_own.at[eight(ring(z, i, nz))], v_all.at[owner, corner], V, z_peer(i))
+
+    def near_v(i, owner):
+        return send(v_own.at[eight(ring(z, i, nz))], v_all.at[owner, corner], V, z_peer(i), v_sem.at[close.index(i)])
+
+    for i in close:
+        near_v(i, z).start()
 
     pad = jnp.zeros((e_hi.shape[1], e_hi.shape[2] - width), bf16)
     for i in range(ny):
@@ -180,11 +187,6 @@
     own_half = pl.ds(pl.multiple_of(core * (r // CORES), r // CORES), r // CORES)
     for i in range(ny):
         if i == ny - 1:
-            all_in(v_all.at[pl.ds(0, nz - 1), corner], V)
-            part = v_all.at[:, corner]
-            for other in (partner, across, (across[0] + 1 - 2 * core, col)):
-                send(part, part, V2, other).start()
-
             all_in(g_all.at[pl.ds(0, GROUP * (nt - 1))], G1)
             g_own[...] = g_all[...].T
             g_t[z, xh, own_half] = g_own[own_half, :]
@@ -203,6 +205,12 @@
         for side in range(XL):
             q_cat[:, side * block:(side + 1) * block] = q_all[XL * place + side]
         x_cat[i] = stacked(q_cat[...])
+        if i == 0:
+            for k in close:
+                near_v(k, ring(z, nz - k, nz)).wait_recv()
+            for k in range(3, nz - 2):
+                v_send(k, z).start()
+
         for k in range(2):
             rotate(i, cuts[k], cuts[k + 1])
             if i == ny - 1:
@@ -266,6 +274,11 @@
                 for side in range(2):
                     t_hi[side, i, to, :] = hi[side * LANES:(side + 1) * LANES]
                     t_lo[side, i, to, :] = lo[side * LANES:(side + 1) * LANES]
+
+    all_in(v_all.at[pl.ds(0, nz - 1 - len(close)), corner], V)
+    part = v_all.at[:, corner]
+    for other in (partner, across, diagonal):
+        send(part, part, V2, other).start()
 
     transpose(0, chunks * 3 // 4)
     for k in range(2):
@@ -450,7 +463,7 @@
         v((block, ntrain), f32), v((block, ntrain), bf16), v((block, ntrain), bf16),
         v((GROUP * nt, r), f32), v((r, LANES), f32), v((nz, XH, r, LANES), f32),
         v((nz, XH, 1, LANES), f32), v((CORES * nz, XH, 1, LANES), f32), v((XH, 1, LANES), f32), v((nt, 1, LANES), f32),
-        dma((ny,)), dma((4,)), dma((2, 12)), dma((ny,)), dma((2, 2)), dma((4, 2)), dma((2, 2)), dma((2, 8)),
+        dma((ny,)), dma((4,)), dma((2, 12)), dma((4,)), dma((ny,)), dma((2, 2)), dma((4, 2)), dma((2, 2)), dma((2, 8)),
     ]
     preconditioned, scores = pl.pallas_call(
         functools.partial(kernel, nrow, ncol),

time: 60.9 us -> 58.6 us (0.962)
  Pallas kernels: 59.1 us -> 56.7 us
    pallas_call x1, Pallas kernels: 59.1 us -> 56.7 us  [shards(): pl.pallas_call(functools.partial(kernel, nrow, ncol), out_shape=(pltpu.VM...]
where the time goes in v4:
time: 58.6 us; the launch traced here: 58.5 us
  Pallas kernels  56.7 us (97%)
  local copies, waits for them, and re-layouts  1.13 us (2%)
  between operations  0.64 us (1%)
    pallas_call x1, Pallas kernels, shards(): pl.pallas_call(functools.partial(kernel, nrow, ncol), out_shape=(pltpu.VM...  56.7 us

profile of v4, /device:TPU:1, one launch (start us, length us, event | category | flops | bytes accessed | tf_op | source)
XLA Modules:
  0.0 58.5 jit_solution(7168163744785317850)
XLA Ops:
  0.6 56.7 %shard_map.68 = (f32[64,100]{1,0:T(8,128)S(1)}, f32[8,128]{1,0:T(8,128)S(1)}) custom-call(f32[64,100]{1,0:T(8,128)} %bitcast.8, f32[800,3200]{1,0:T(8,128)} %e_ref.1, f32[64,100]{1,0:T(8,128)} %bitcast.9, f32[100,2048]{1,0:T(8,128)} %bitcast.7, f32[8,64]{1,0:T(8,128)} %g_ref.1), custom_call_target="tpu_custom_call" | custom-call | tf_op jit(solution)/shard_map/pallas_call | solution.py:468
  57.4 0.6 %copy.8 = f32[100,64]{0,1:T(8,128)} copy(f32[100,64]{0,1:T(8,128)S(1)} %bitcast.6) | data formatting | bytes 51200
  58.0 0.5 slice_bitcast_fusion

commit v5 on v4

--- a/solution.py
+++ b/solution.py
@@ -11,6 +11,7 @@
 MESH = pl.DeviceIdType.MESH
 f32, bf16 = jnp.float32, jnp.bfloat16
 LANES, GROUP = 128, 8
+CHUNKS = 3
 CORES = XH = 2
 XL = 2
 
@@ -53,7 +54,7 @@
     partner = (row + 1 - 2 * core, col)
     across = (row + 2 - 4 * xh, col)
     near = sorted(range(ny), key=lambda d: min(d, ny - d))
-    Q, G1, V, V2, AG, FW, G2, G3, G4, P_, F1, F2 = range(12)
+    Q, G1, V, V2, AG, FW, FW_LAST, G2, G3, G4, P_, F1, F2 = range(13)
     corner = XH * xh + core
 
     def send(src, dst, kind, device, recv=None):
@@ -182,20 +183,10 @@
                 else:
                     rot[side, :, to] += part
 
-    cuts = (0, chunks // 2 + 1, chunks)
+    cuts = [-(-chunks * k // CHUNKS) for k in range(CHUNKS + 1)]
     c_copies = []
     own_half = pl.ds(pl.multiple_of(core * (r // CORES), r // CORES), r // CORES)
     for i in range(ny):
-        if i == ny - 1:
-            all_in(g_all.at[pl.ds(0, GROUP * (nt - 1))], G1)
-            g_own[...] = g_all[...].T
-            g_t[z, xh, own_half] = g_own[own_half, :]
-
-            @pl.loop(1, nz)
-            def _(k):
-                part = g_t.at[z, xh, own_half]
-                send(part, part, G2, z_peer(k)).start()
-
         place = ring(y, near[i], ny)
         if i == 0:
             there = q_all.at[pl.ds(XL * place + 1 - xl, 1)]
@@ -211,7 +202,7 @@
             for k in range(3, nz - 2):
                 v_send(k, z).start()
 
-        for k in range(2):
+        for k in range(len(cuts) - 1):
             rotate(i, cuts[k], cuts[k + 1])
             if i == ny - 1:
                 at = pl.ds(cuts[k] * LANES, (cuts[k + 1] - cuts[k]) * LANES)
@@ -280,13 +271,19 @@
     for other in (partner, across, diagonal):
         send(part, part, V2, other).start()
 
-    transpose(0, chunks * 3 // 4)
-    for k in range(2):
+    all_in(g_all.at[pl.ds(0, GROUP * (nt - 1))], G1)
+    g_own[...] = g_all[...].T
+    g_t[z, xh, own_half] = g_own[own_half, :]
+
+    transpose(0, chunks // 2 + 1)
+    for k in range(len(lanes)):
         through(k)
-    all_in(g_t.at[pl.ds(0, nz - 1), xh, own_half], G2)
-    part = g_t.at[:, xh, own_half]
-    send(part, part, G3, across).start()
-    transpose(chunks * 3 // 4, chunks)
+    @pl.loop(1, nz)
+    def _(k):
+        part = g_t.at[z, xh, own_half]
+        send(part, part, G2, z_peer(k)).start()
+
+    transpose(chunks // 2 + 1, chunks - 2)
 
     def x_copy(k):
         at = lanes[k]
@@ -299,9 +296,9 @@
         part = s_all.at[core, eight(owner), at]
         return send(part, part, AG, z_peer(i), ag_sem.at[k, kind])
 
-    def fw_send(owner, at):
+    def fw_send(owner, at, k):
         part = s_all.at[core, eight(owner), at]
-        return send(part, part, FW, partner)
+        return send(part, part, FW_LAST if k == CHUNKS - 1 else FW, partner)
 
     for k, at in enumerate(lanes):
         there = z_in.at[:, :, at]
@@ -315,6 +312,7 @@
     for j in range(2 * chunks):
         v_use[j % 2, :, (j // 2) * LANES:(j // 2 + 1) * LANES] = v_cat[:, j * LANES:(j + 1) * LANES]
 
+    transpose(chunks - 2, chunks)
     all_out(q_all.at[pl.ds(0, ncol - 1)], Q)
     all_out(g_all.at[pl.ds(0, GROUP * (nt - 1))], G1)
     all_out(v_all.at[pl.ds(0, nz - 1), corner], V)
@@ -336,7 +334,7 @@
         s_all[core, eight(z), at] = (x_out[:, at] + x_in[:, at]) / (v_use[core, :, at] + damping)
         for step, way in ways:
             ag_send(2 * step % nz, z, at, k, 2 + way).start()
-        fw_send(z, at).start()
+        fw_send(z, at, k).start()
 
     for k, at in enumerate(lanes):
         for step, way in ways:
@@ -348,37 +346,51 @@
             ag_send(1, owner, at, k, 2 + way).wait_recv()
             ag_send(2 * step % nz, owner, halves[k][way], k, 6 + way).start()
             ag_send(step, owner, at, k, 4 + way).start()
-            fw_send(owner, at).start()
+            fw_send(owner, at, k).start()
         if k == 0:
-            all_in(g_t.at[:, 1 - xh, own_half], G3)
-            part = g_t.at[:, :, own_half]
-            send(part, part, G4, partner).start()
+            all_in(g_t.at[pl.ds(0, nz - 1), xh, own_half], G2)
+            part = g_t.at[:, xh, own_half]
+            send(part, part, G3, across).start()
+
+    early, late = pl.ds(0, cuts[-2] * LANES), lanes[-1]
+
+    def back(side, i, at):
+        return folded(
+            jnp.dot(s_cat[side, :, at], t_hi[side, i, at, :], preferred_element_type=f32)
+            + jnp.dot(s_cat[side, :, at], t_lo[side, i, at, :], preferred_element_type=f32)
+        )
 
     for k, at in enumerate(lanes):
         for away, kind in ((1, 0), (3, 4)):
             for step, way in ways:
                 owner = ring(z, nz - away * step % nz, nz)
                 ag_send(1, owner, at, k, kind + way).wait_recv()
-                fw_send(owner, at).start()
+                fw_send(owner, at, k).start()
         for step, way in ways:
             owner = ring(z, nz // 2, nz)
             ag_send(1, owner, halves[k][way], k, 6 + way).wait_recv()
-            fw_send(owner, halves[k][way]).start()
-
-    def back(side, i):
-        return folded(
-            jnp.dot(s_cat[side], t_hi[side, i], preferred_element_type=f32)
-            + jnp.dot(s_cat[side], t_lo[side, i], preferred_element_type=f32)
-        )
-
-    s_cat[core] = stacked(s_all[core])
+            fw_send(owner, halves[k][way], k).start()
+
+        if k == CHUNKS - 2:
+            s_cat[core, :, early] = stacked(s_all[core, :, early])
+            for i in range(ny):
+                p_own[i] = back(core, i, early)
+
+    s_cat[core, :, late] = stacked(s_all[core, :, late])
     for i in range(ny):
-        p_own[i] = back(core, i)
-    all_in(s_all.at[1 - core], FW)
-    s_cat[1 - core] = stacked(s_all[1 - core])
+        p_own[i] += back(core, i, late)
+    all_in(g_t.at[:, 1 - xh, own_half], G3)
+    part = g_t.at[:, :, own_half]
+    send(part, part, G4, partner).start()
+    all_in(s_all.at[1 - core, :, early], FW)
+    s_cat[1 - core, :, early] = stacked(s_all[1 - core, :, early])
+    for i in range(ny):
+        p_own[i] += back(1 - core, i, early)
+    all_in(s_all.at[1 - core, :, late], FW_LAST)
+    s_cat[1 - core, :, late] = stacked(s_all[1 - core, :, late])
     for group in ((3, 2), (1, 0)):
         for i in group:
-            part = p_own[i] + back(1 - core, i)
+            part = p_own[i] + back(1 - core, i, late)
             for side in range(XL):
                 p_out[i, side] = part[:, side * block:(side + 1) * block]
         for i in group:
@@ -392,7 +404,8 @@
     all_in(g_t.at[:, :, pl.ds(pl.multiple_of((1 - core) * (r // CORES), r // CORES), r // CORES)], G4)
     all_out(g_t.at[pl.ds(0, nz - 1), xh, own_half], G2)
     all_out(s_all.at[core, pl.ds(0, GROUP * (nz - 1))], AG)
-    all_out(s_all.at[core], FW)
+    all_out(s_all.at[core, :, early], FW)
+    all_out(s_all.at[core, :, late], FW_LAST)
     all_out(g_t.at[:, xh, own_half], G3)
     all_out(g_t.at[:, :, own_half], G4)
 
@@ -463,7 +476,7 @@
         v((block, ntrain), f32), v((block, ntrain), bf16), v((block, ntrain), bf16),
         v((GROUP * nt, r), f32), v((r, LANES), f32), v((nz, XH, r, LANES), f32),
         v((nz, XH, 1, LANES), f32), v((CORES * nz, XH, 1, LANES), f32), v((XH, 1, LANES), f32), v((nt, 1, LANES), f32),
-        dma((ny,)), dma((4,)), dma((2, 12)), dma((4,)), dma((ny,)), dma((2, 2)), dma((4, 2)), dma((2, 2)), dma((2, 8)),
+        dma((ny,)), dma((4,)), dma((2, 13)), dma((4,)), dma((ny,)), dma((2, CHUNKS)), dma((4, CHUNKS)), dma((2, CHUNKS)), dma((CHUNKS, 8)),
     ]
     preconditioned, scores = pl.pallas_call(
         functools.partial(kernel, nrow, ncol),

time: 58.6 us -> 57.4 us (0.980)
  Pallas kernels: 56.7 us -> 55.5 us
    pallas_call x1, Pallas kernels: 56.7 us -> 55.5 us  [shards(): pl.pallas_call(functools.partial(kernel, nrow, ncol), out_shape=(pltpu.VM...]
where the time goes in v5:
time: 57.4 us; the launch traced here: 57.3 us
  Pallas kernels  55.5 us (97%)
  local copies, waits for them, and re-layouts  1.13 us (2%)
  between operations  0.64 us (1%)
    pallas_call x1, Pallas kernels, shards(): pl.pallas_call(functools.partial(kernel, nrow, ncol), out_shape=(pltpu.VM...  55.5 us

profile of v5, /device:TPU:1, one launch (start us, length us, event | category | flops | bytes accessed | tf_op | source)
XLA Modules:
  0.0 57.3 jit_solution(17987286302711456939)
XLA Ops:
  0.6 55.5 %shard_map.68 = (f32[64,100]{1,0:T(8,128)S(1)}, f32[8,128]{1,0:T(8,128)S(1)}) custom-call(f32[64,100]{1,0:T(8,128)} %bitcast.8, f32[800,3200]{1,0:T(8,128)} %e_ref.1, f32[64,100]{1,0:T(8,128)} %bitcast.9, f32[100,2048]{1,0:T(8,128)} %bitcast.7, f32[8,64]{1,0:T(8,128)} %g_ref.1), custom_call_target="tpu_custom_call" | custom-call | tf_op jit(solution)/shard_map/pallas_call | solution.py:481
  56.1 0.6 %copy.8 = f32[100,64]{0,1:T(8,128)} copy(f32[100,64]{0,1:T(8,128)S(1)} %bitcast.6) | data formatting | bytes 51200
  56.8 0.5 slice_bitcast_fusion

commit v6 on v5

--- a/solution.py
+++ b/solution.py
@@ -37,7 +37,7 @@
     stage, e_hi, e_lo, t_hi, t_lo, q_all, q_cat, x_cat, rot, rot_in, mine, z_far, z_mid, z_out, z_in, x_out, x_in,
     v_own, v_all, v_cat, v_use, s_all, s_cat, p_own, p_out, p_in,
     a_own, a_hi, a_lo, g_all, g_own, g_t, f_out, f_in, f_sum, f_all,
-    e_sem, local, one_sem, v_sem, q_sem, c_sem, z_sem, x_sem, ag_sem,
+    e_sem, local, far_sem, one_sem, v_sem, q_sem, c_sem, z_sem, x_sem, ag_sem,
 ):
     row, col = lax.axis_index("row"), lax.axis_index("col")
     core, chip = lax.rem(row, CORES), lax.div(row, CORES)
@@ -98,13 +98,10 @@
 
     close = (1, nz - 1, 2, nz - 2)
 
-    @pl.loop(1, ncol)
-    def _(i):
-        other = ring(col, i, ncol)
-        pl.semaphore_signal(barrier, inc=1, device_id=(row, other), device_id_type=MESH)
-        pl.semaphore_signal(barrier, inc=1, device_id=(partner[0], other), device_id_type=MESH)
-
-    for device in (*(z_peer(i) for i in close), across, diagonal, partner):
+    beside = [XL * ring(y, d, ny) + side for d in near[1:-1] for side in range(XL)] + [col + 1 - 2 * xl]
+    greeted = [(there, other) for other in beside for there in (row, partner[0])]
+    greeted += [*(z_peer(i) for i in close), across, diagonal, partner]
+    for device in greeted:
         pl.semaphore_signal(barrier, inc=1, device_id=device, device_id_type=MESH)
 
     def convert(i):
@@ -127,7 +124,8 @@
     q_copy.wait()
     g_copy.wait()
     v_copy.wait()
-    pl.semaphore_wait(barrier, 2 * (ncol - 1) + len(close) + 3)
+    pl.semaphore_wait(barrier, len(greeted))
+    pl.semaphore_signal(far_sem, inc=1, device_id=(row, XL * ring(y, 1, ny) + xl), device_id_type=MESH)
 
     own_q = q_all.at[col]
     send(own_q, own_q, Q, (row, col + 1 - 2 * xl), q_sem.at[0]).start()
@@ -139,14 +137,6 @@
                 send(own_q, own_q, Q, (row, XL * ring(y, d, ny) + side), q_sem.at[slot]).start()
 
     q_send(near[1:-1])
-
-    @pl.loop(1, nt)
-    def _(i):
-        to = ring(t, i, nt)
-        part = g_all.at[eight(t)]
-        send(part, part, G1, (CORES * chip + lax.div(to, ncol), lax.rem(to, ncol))).start()
-
-    q_send(near[-1:])
 
     def v_send(i, owner):
         return send(v_own.at[eight(ring(z, i, nz))], v_all.at[owner, corner], V, z_peer(i))
@@ -164,7 +154,18 @@
     q_cat[:, XL * block:] = jnp.zeros((r, q_cat.shape[1] - XL * block), f32)
     v_cat[:, block * nrow:] = jnp.zeros((GROUP, v_cat.shape[1] - block * nrow), f32)
     v_all[z, corner] = v_own[eight(z), :]
-    for i in range(ny):
+    for i in range(2):
+        convert(i)
+    pl.semaphore_wait(far_sem, 1)
+    q_send(near[-1:])
+
+    @pl.loop(1, nt)
+    def _(i):
+        to = ring(t, i, nt)
+        part = g_all.at[eight(t)]
+        send(part, part, G1, (CORES * chip + lax.div(to, ncol), lax.rem(to, ncol))).start()
+
+    for i in range(2, ny):
         convert(i)
 
     def rotate(i, first, last):
@@ -413,24 +414,24 @@
     whole = lax.fori_loop(1, ncol, lambda i, total: total + p_in[ring(col, i, ncol)], p_out[0, xl])
     p_ref[...] = whole
 
+    place, nplace = CORES * z + core, CORES * nz
     x = stacked(whole)
-    for k in range(nchip // 2):
-        at = slice(k * pair, (k + 1) * pair)
-        projected = folded(
-            jnp.dot(x, a_hi[:, at], preferred_element_type=f32) + jnp.dot(x, a_lo[:, at], preferred_element_type=f32)
-        )
-        for side in range(2):
-            there = 2 * k + side
-            part = projected[:, side * LANES:(side + 1) * LANES] * g_t[there // XH, there % XH]
-            f_out[there // XH, there % XH] = jnp.sum(part, axis=0, keepdims=True)
-
-    place, nplace = CORES * z + core, CORES * nz
-
-    @pl.loop(1, nplace)
-    def _(i):
-        to = ring(place, i, nplace)
-        there = lax.div(to, CORES)
-        send(f_out.at[there], f_in.at[place], F1, (CORES * (XH * there + xh) + lax.rem(to, CORES), col)).start()
+    far = sorted(range(nz), key=lambda i: -min(i, nz - i))
+    for group in (far[:nz // 2], far[nz // 2:]):
+        for i in group:
+            there = ring(z, i, nz)
+            at = pl.ds(pl.multiple_of(there * pair, pair), pair)
+            projected = folded(
+                jnp.dot(x, a_hi[:, at], preferred_element_type=f32)
+                + jnp.dot(x, a_lo[:, at], preferred_element_type=f32)
+            )
+            for side in range(XH):
+                part = projected[:, side * LANES:(side + 1) * LANES] * g_t[there, side]
+                f_out[there, side] = jnp.sum(part, axis=0, keepdims=True)
+        for i in group:
+            there = ring(z, i, nz)
+            for other in range(CORES) if i else (1 - core,):
+                send(f_out.at[there], f_in.at[place], F1, (CORES * (XH * there + xh) + other, col)).start()
 
     all_out(p_in.at[pl.ds(0, ncol - 1)], P_)
     all_in(f_in.at[pl.ds(0, nplace - 1)], F1)
@@ -476,7 +477,7 @@
         v((block, ntrain), f32), v((block, ntrain), bf16), v((block, ntrain), bf16),
         v((GROUP * nt, r), f32), v((r, LANES), f32), v((nz, XH, r, LANES), f32),
         v((nz, XH, 1, LANES), f32), v((CORES * nz, XH, 1, LANES), f32), v((XH, 1, LANES), f32), v((nt, 1, LANES), f32),
-        dma((ny,)), dma((4,)), dma((2, 13)), dma((4,)), dma((ny,)), dma((2, CHUNKS)), dma((4, CHUNKS)), dma((2, CHUNKS)), dma((CHUNKS, 8)),
+        dma((ny,)), dma((4,)), pltpu.SemaphoreType.REGULAR, dma((2, 13)), dma((4,)), dma((ny,)), dma((2, CHUNKS)), dma((4, CHUNKS)), dma((2, CHUNKS)), dma((CHUNKS, 8)),
     ]
     preconditioned, scores = pl.pallas_call(
         functools.partial(kernel, nrow, ncol),

time: 57.4 us -> 57 us (level)
  no operation moved by 1% of the time
where the time goes in v6:
time: 57 us; the launch traced here: 56.9 us
  Pallas kernels  55.1 us (97%)
  local copies, waits for them, and re-layouts  1.13 us (2%)
  between operations  0.64 us (1%)
    pallas_call x1, Pallas kernels, shards(): pl.pallas_call(functools.partial(kernel, nrow, ncol), out_shape=(pltpu.VM...  55.1 us

profile of v6, /device:TPU:1, one launch (start us, length us, event | category | flops | bytes accessed | tf_op | source)
XLA Modules:
  0.0 56.9 jit_solution(8694191608635194588)
XLA Ops:
  0.6 55.1 %shard_map.68 = (f32[64,100]{1,0:T(8,128)S(1)}, f32[8,128]{1,0:T(8,128)S(1)}) custom-call(f32[64,100]{1,0:T(8,128)} %bitcast.8, f32[800,3200]{1,0:T(8,128)} %e_ref.1, f32[64,100]{1,0:T(8,128)} %bitcast.9, f32[100,2048]{1,0:T(8,128)} %bitcast.7, f32[8,64]{1,0:T(8,128)} %g_ref.1), custom_call_target="tpu_custom_call" | custom-call | tf_op jit(solution)/shard_map/pallas_call | solution.py:482
  55.8 0.6 %copy.8 = f32[100,64]{0,1:T(8,128)} copy(f32[100,64]{0,1:T(8,128)S(1)} %bitcast.6) | data formatting | bytes 51200
  56.4 0.5 slice_bitcast_fusion
